TPU v7x, 32 devices: a whole 2x2x4 slice. The times are simulated.
32 devices in a mesh: samp: 32 (over z, y, x, core), var: 1.
Axes of the slice: x: 2, y: 2, z: 4, core: 2. Of those that a mesh axis runs over, the one named last changes fastest.
Arguments:
- phenotype: float32 [32768], replicated, may hold values from -6 to 6
- perm_index: int32 [64, 32768], P(None, 'samp'), may hold values from 0 to 32767, each once within a row
- genotypes: bfloat16 [32768, 2048], P('samp', 'var'), may hold values from 0 to 2
Outputs:
- statistics: float32 [64, 2048], P('samp', 'var')
- largest: float32 [64], P('samp')
Inputs may be any that keep to these rules, and one draw needn't show every extreme that they name: Each row of perm_index is a permutation of 0 to 32767.
All inputs are finite; a program needn't handle non-finite values.
Results may differ from a plain program's by a relative error of at most 0.003.
Values sent between devices are 32-bit elements; how exact they have to be, the bound alone decides.
No kernel may reach another device: no remote copies, remote signals or barrier semaphores. Data moves between devices by JAX's collectives and lax.ppermute only.
A program may use at most 64 MiB of HBM per device.

v0:
```python
import jax
import jax.numpy as jnp
from jax import lax
from jax.sharding import PartitionSpec as P


def on_device(phenotype, perm_index, genotypes):
    centred = phenotype - jnp.mean(phenotype)
    sigma2 = jnp.mean(centred * centred) + 1e-05
    local_count = perm_index.shape[1]
    perm_total = perm_index.shape[0]
    table = centred.astype(jnp.bfloat16).reshape(centred.shape[0] // 128, 128)

    def select_rows(index_rows):
        upper_part = jax.nn.one_hot(index_rows // 128, table.shape[0], dtype=jnp.bfloat16)
        picked = jnp.einsum("pnh,hc->pnc", upper_part, table, preferred_element_type=jnp.float32)
        lower_part = jax.nn.one_hot(index_rows % 128, 128, dtype=jnp.float32)
        return jnp.sum(picked * lower_part, axis=-1).astype(jnp.bfloat16)

    grouped = perm_index.reshape(perm_total // 8, 8, local_count)
    permuted = lax.map(select_rows, grouped).reshape(perm_total, local_count)
    ones_row = jnp.ones((1, genotypes.shape[0]), jnp.bfloat16)
    count_row = jnp.dot(ones_row, genotypes, preferred_element_type=jnp.float32)
    square_row = jnp.einsum("ij,ij->j", genotypes, genotypes, preferred_element_type=jnp.float32)[
        None, :
    ]
    moments = jnp.concatenate([count_row, square_row], axis=0)
    block_rows = perm_total // lax.axis_size("samp")
    samples = local_count * lax.axis_size("samp")
    partial_value = jnp.dot(permuted, genotypes, preferred_element_type=jnp.float32)
    scores, totals = lax.psum((partial_value, moments), "samp")
    own_scores = lax.dynamic_slice_in_dim(
        scores, lax.axis_index("samp") * block_rows, block_rows, 0
    )
    spread = totals[1] - totals[0] * totals[0] / samples + 1.0
    statistic = own_scores / jnp.sqrt(sigma2 * spread)[None, :]
    largest = lax.pmax(jnp.max(jnp.abs(statistic), axis=1), "var")
    return (statistic, largest)


def solution(mesh):
    placed = (P(), P(None, "samp"), P("samp", "var"))
    return jax.shard_map(
        on_device,
        mesh=mesh,
        in_specs=placed,
        out_specs=(P("samp", "var"), P("samp")),
        check_vma=False,
    )
```

profile of v0, /device:TPU:0, one launch (start us, length us, event | category | flops | bytes accessed | tf_op | source)
XLA Modules:
  0.0 190.2 jit_solution(13008138082691047050)
XLA Ops:
  7.2 1.5 reduce_sum.30
  9.4 1.5 fusion.9
  11.1 34.3 %while.12 = (s32[]{:T(128)}, bf16[8,8,1024]{2,1,0:T(8,128)(2,1)S(1)}, s32[8,8,1024]{2,1,0:T(8,128)}, bf16[256,128]{0,1:T(8,128)(2,1)S(1)}, s32[]{:T(128)}) while((s32[]{:T(128)}, bf16[8,8,1024]{2,1,0:T(8,128)(2,1)S(1)}, s32[8,8,1024]{2,1,0:T(8,128)}, bf16[256,128]{0,1:T(8,128)(2,1)S(1)}, s32[]{:T(128)}) %tuple.41), condition=%wide.region_3.4_spmd, body=%wide.region_1.3_spmd.sunk | while | flops 542310400 | bytes 327753 | solution.py:21
  11.1 0.8 add_select_fusion.4
  12.7 2.7 %select_reduce_fusion.2 = bf16[8,1024]{1,0:T(8,128)(2,1)S(1)} fusion(s32[8,1024]{1,0:T(8,128)S(1)} %add_select_fusion.5, s32[8,1024]{1,0:T(8,128)S(1)} %get-tuple-element.105, bf16[256,128]{0,1:T(8,128)(2,1)S(1)} %get-tuple-element.119), kind=kOutput, calls=%fused_computation.2.clone.1 | convolution fusion | flops 542105600 | bytes 147456 | tf_op jit(solution)/shard_map/while/body/eval_jaxpr/pnh,hc->pnc/dot_general | solution.py:16
  15.4 0.8 add_select_fusion.4
  16.9 2.7 %select_reduce_fusion.2 = bf16[8,1024]{1,0:T(8,128)(2,1)S(1)} fusion(s32[8,1024]{1,0:T(8,128)S(1)} %add_select_fusion.5, s32[8,1024]{1,0:T(8,128)S(1)} %get-tuple-element.105, bf16[256,128]{0,1:T(8,128)(2,1)S(1)} %get-tuple-element.119), kind=kOutput, calls=%fused_computation.2.clone.1 | convolution fusion | flops 542105600 | bytes 147456 | tf_op jit(solution)/shard_map/while/body/eval_jaxpr/pnh,hc->pnc/dot_general | solution.py:16
  19.7 0.8 add_select_fusion.4
  21.2 2.7 %select_reduce_fusion.2 = bf16[8,1024]{1,0:T(8,128)(2,1)S(1)} fusion(s32[8,1024]{1,0:T(8,128)S(1)} %add_select_fusion.5, s32[8,1024]{1,0:T(8,128)S(1)} %get-tuple-element.105, bf16[256,128]{0,1:T(8,128)(2,1)S(1)} %get-tuple-element.119), kind=kOutput, calls=%fused_computation.2.clone.1 | convolution fusion | flops 542105600 | bytes 147456 | tf_op jit(solution)/shard_map/while/body/eval_jaxpr/pnh,hc->pnc/dot_general | solution.py:16
  23.9 0.8 add_select_fusion.4
  25.5 2.7 %select_reduce_fusion.2 = bf16[8,1024]{1,0:T(8,128)(2,1)S(1)} fusion(s32[8,1024]{1,0:T(8,128)S(1)} %add_select_fusion.5, s32[8,1024]{1,0:T(8,128)S(1)} %get-tuple-element.105, bf16[256,128]{0,1:T(8,128)(2,1)S(1)} %get-tuple-element.119), kind=kOutput, calls=%fused_computation.2.clone.1 | convolution fusion | flops 542105600 | bytes 147456 | tf_op jit(solution)/shard_map/while/body/eval_jaxpr/pnh,hc->pnc/dot_general | solution.py:16
  28.2 0.8 add_select_fusion.4
  29.8 2.7 %select_reduce_fusion.2 = bf16[8,1024]{1,0:T(8,128)(2,1)S(1)} fusion(s32[8,1024]{1,0:T(8,128)S(1)} %add_select_fusion.5, s32[8,1024]{1,0:T(8,128)S(1)} %get-tuple-element.105, bf16[256,128]{0,1:T(8,128)(2,1)S(1)} %get-tuple-element.119), kind=kOutput, calls=%fused_computation.2.clone.1 | convolution fusion | flops 542105600 | bytes 147456 | tf_op jit(solution)/shard_map/while/body/eval_jaxpr/pnh,hc->pnc/dot_general | solution.py:16
  32.5 0.8 add_select_fusion.4
  34.1 2.7 %select_reduce_fusion.2 = bf16[8,1024]{1,0:T(8,128)(2,1)S(1)} fusion(s32[8,1024]{1,0:T(8,128)S(1)} %add_select_fusion.5, s32[8,1024]{1,0:T(8,128)S(1)} %get-tuple-element.105, bf16[256,128]{0,1:T(8,128)(2,1)S(1)} %get-tuple-element.119), kind=kOutput, calls=%fused_computation.2.clone.1 | convolution fusion | flops 542105600 | bytes 147456 | tf_op jit(solution)/shard_map/while/body/eval_jaxpr/pnh,hc->pnc/dot_general | solution.py:16
  36.8 0.8 add_select_fusion.4
  38.4 2.7 %select_reduce_fusion.2 = bf16[8,1024]{1,0:T(8,128)(2,1)S(1)} fusion(s32[8,1024]{1,0:T(8,128)S(1)} %add_select_fusion.5, s32[8,1024]{1,0:T(8,128)S(1)} %get-tuple-element.105, bf16[256,128]{0,1:T(8,128)(2,1)S(1)} %get-tuple-element.119), kind=kOutput, calls=%fused_computation.2.clone.1 | convolution fusion | flops 542105600 | bytes 147456 | tf_op jit(solution)/shard_map/while/body/eval_jaxpr/pnh,hc->pnc/dot_general | solution.py:16
  41.1 0.8 add_select_fusion.4
  42.7 2.7 %select_reduce_fusion.2 = bf16[8,1024]{1,0:T(8,128)(2,1)S(1)} fusion(s32[8,1024]{1,0:T(8,128)S(1)} %add_select_fusion.5, s32[8,1024]{1,0:T(8,128)S(1)} %get-tuple-element.105, bf16[256,128]{0,1:T(8,128)(2,1)S(1)} %get-tuple-element.119), kind=kOutput, calls=%fused_computation.2.clone.1 | convolution fusion | flops 542105600 | bytes 147456 | tf_op jit(solution)/shard_map/while/body/eval_jaxpr/pnh,hc->pnc/dot_general | solution.py:16
  45.4 3.8 %fusion.7 = f32[64,2048]{1,0:T(8,128)} fusion(bf16[1024,2048]{1,0:T(8,128)(2,1)} %param.7, bf16[8,8,1024]{2,1,0:T(8,128)(2,1)S(1)} %get-tuple-element.58), kind=kOutput, calls=%fused_computation.19 | convolution fusion | flops 268435456 | bytes 4849664 | tf_op jit(solution)/shard_map/dot_general | solution.py:30
  49.3 3.2 %fusion.6 = f32[2048]{0:T(1024)S(1)} fusion(bf16[1024,2048]{1,0:T(8,128)(2,1)} %param.7), kind=kLoop, calls=%fused_computation.18 | loop fusion | flops 6289408 | bytes 4202496 | tf_op jit(solution)/shard_map/ij,ij->j/dot_general | solution.py:24
  54.0 42.0 %psum.15 = f32[2,2048]{1,0:T(2,128)S(1)} all-reduce(f32[2,2048]{1,0:T(2,128)S(1)} %pad_maximum_fusion), channel_id=1, replica_groups=mesh['samp'=32,'var'=1] {'samp'}, use_global_device_ids=true, to_apply=%region_6.7 | all-reduce | flops 4096 | bytes 32768 | tf_op jit(solution)/shard_map/psum | solution.py:31
  96.1 85.1 %all-reduce.2.cloned.1.call-done = f32[64,2048]{1,0:T(8,128)} async-done(((f32[64,2048]{1,0:T(8,128)}), f32[64,2048]{1,0:T(8,128)}) %all-reduce.2.cloned.1.call-update) | async-done | bytes 524304 | tf_op jit(solution)/shard_map/psum | solution.py:31
  181.2 2.1 %abs_reduce_fusion = (f32[2]{0:T(128)}, f32[2,2048]{1,0:T(2,128)}) fusion(f32[2048]{0:T(1024)S(1)} %bitcast.52, f32[64,2048]{1,0:T(8,128)} %all-reduce.2.cloned.1.call-done, s32[]{:T(128)S(6)} %select_n.31), kind=kLoop, calls=%fused_computation.25 | loop fusion | flops 12286 | bytes 40972 | tf_op jit(solution)/shard_map/reduce_max | solution.py:37
  (25 shorter events, 7.4 us)
Async XLA Ops:
  7.2 174.1 %all-reduce.2.cloned.1.call-start = ((), (), s32[]{:S(2)}) async-start(), calls=%async_computation | async-start | bytes 1048576 | tf_op jit(solution)/shard_map/psum | solution.py:31
  49.2 3.5 %copy-start = (bf16[1024,2048]{1,0:T(8,128)(2,1)S(1)}, bf16[1024,2048]{1,0:T(8,128)(2,1)}, u32[]{:S(2)}) copy-start(bf16[1024,2048]{1,0:T(8,128)(2,1)} %param.7) | copy-start | bytes 12582916
Sparse Core Ops, SparseCore 0:
  49.4 131.8 all-reduce.1
where the time goes:
time: 192 us; the launch traced here: 190 us
  waiting for transfers between devices  85.1 us (44%)
  blocking collectives  42 us (22%)
  matrix products  25.9 us (13%)
  other arithmetic  21 us (11%)
  between operations  15.4 us (8%)
    psum x1, waiting for transfers between devices, on_device(): scores, totals = lax.psum((partial_value, moments), 'samp')  85.1 us
    psum x1, blocking collectives, on_device(): scores, totals = lax.psum((partial_value, moments), 'samp')  42 us
    dot_general x8, matrix products, select_rows(): jnp.einsum('pnh,hc->pnc', upper_part, table, preferred_element_type=jnp.f...  21.4 us
    select_n x8, other arithmetic, select_rows(): index_rows // 128  6.3 us
    select_n x8, other arithmetic, select_rows(): lower_part = jax.nn.one_hot(index_rows % 128, 128, dtype=jnp.float32)  6.25 us
    dot_general x1, matrix products, on_device(): jnp.dot(permuted, genotypes, preferred_element_type=jnp.float32)  3.84 us
  transfers between devices with their start and end apart: 1, of which 1 were waited for; matrix products, arithmetic and copies ran while one was open for 2% of the time, Pallas kernels for 0%

commit v1 on v0

v1 whole, which is shorter than its diff:
```python
import functools

import jax
import jax.numpy as jnp
from jax import lax
from jax.experimental import pallas as pl
from jax.experimental.pallas import tpu as pltpu
from jax.sharding import PartitionSpec as P

LANES = 128
SUBLANES = 8

LANE_GATHER = lax.GatherDimensionNumbers(
    offset_dims=(),
    collapsed_slice_dims=(1,),
    start_index_map=(1,),
    operand_batching_dims=(0,),
    start_indices_batching_dims=(0,),
)


def round_bits(devices, odd_core):
    bits = list(range(1, devices.bit_length() - 1))
    if odd_core and len(bits) >= 2:
        bits[0], bits[1] = bits[1], bits[0]
    return [0] + bits


def encode(value):
    size = jnp.abs(value)
    exponent = jnp.zeros(value.shape, jnp.int32)
    for step in (64, 32, 16, 8, 4, 2, 1):
        small = size < 2.0 ** (4 - step)
        size = jnp.where(small, size * 2.0**step, size)
        exponent = jnp.where(small, exponent + step, exponent)
    code = (size * 16.0).astype(jnp.int32) + exponent * 256
    return jnp.where(value < 0.0, code + 32768, code)


def decode(code):
    low_exponent = (code >> 8) & 15
    value = ((code & 255) << (15 - low_exponent)).astype(jnp.float32) * 2.0**-19
    for step in (16, 32, 64):
        value = jnp.where((code & (256 * step)) != 0, value * 2.0**-step, value)
    return jnp.where((code & 32768) != 0, -value, value)


def lane_gather(row, lanes):
    return lax.gather(
        row, lanes[..., None], LANE_GATHER, (1, 1), mode=lax.GatherScatterMode.PROMISE_IN_BOUNDS
    )


def look_up(table_ref, index):
    words = table_ref.shape[0]
    lanes = index & (LANES - 1)
    high = index >> 7
    masks = [((high >> k) & 1) != 0 for k in range(words.bit_length() - 1)]
    stack = []
    for word in range(words):
        row = jnp.broadcast_to(table_ref[word : word + 1, :], index.shape)
        value = lane_gather(row, lanes)
        k = 0
        while (word >> k) & 1:
            value = jnp.where(masks[k], value, stack.pop())
            k += 1
        stack.append(value)
    code = jnp.where(high >= words, stack[0] >> 16, stack[0])
    return decode(code)


def source_rows(devices, block_rows, shape, axis):
    me = lax.axis_index("samp")
    row = lax.broadcasted_iota(jnp.int32, shape, axis)
    slot, inner = row // block_rows, row % block_rows
    rounds = devices.bit_length() - 1
    even, odd = (round_bits(devices, side) for side in (False, True))

    def spread(bits):
        owner = jnp.zeros(shape, jnp.int32)
        for k, bit in enumerate(bits):
            owner = owner | (((slot >> (rounds - 1 - k)) & 1) << bit)
        return owner

    upper = (slot >> (rounds - 1)) & 1
    use_odd = ((me & 1) ^ upper) == 1
    owner = me ^ jnp.where(use_odd, spread(odd), spread(even))
    return owner * block_rows + inner


def partial_kernel(devices, block_rows, phenotype_ref, index_ref, genotypes_hbm, out_ref, sigma2_ref,
                   genotypes_ref, table_ref, permuted_ref, semaphores):
    perms, local_count = index_ref.shape
    variants = genotypes_ref.shape[1]
    columns = variants // LANES
    chunks = local_count // LANES
    samples = phenotype_ref.shape[0] * LANES

    def chunk_copy(i):
        rows = pl.ds(pl.multiple_of(i * LANES, LANES), LANES)
        return pltpu.make_async_copy(genotypes_hbm.at[rows], genotypes_ref.at[rows], semaphores.at[i])

    for i in range(chunks):
        chunk_copy(i).start()

    phenotype = phenotype_ref[...]
    centred = phenotype - jnp.sum(phenotype) / samples
    sigma2_ref[0] = jnp.sum(centred * centred) / samples + 1e-05
    code = encode(centred.astype(jnp.bfloat16).astype(jnp.float32))
    words = table_ref.shape[0]
    table_ref[...] = code[:words] | (code[words:] << 16)

    square_rows = (perms + 1) * columns

    def one_chunk(i, square):
        cols = pl.ds(pl.multiple_of(i * LANES, LANES), LANES)
        for block in range(0, perms, 16):
            halves = [
                look_up(table_ref, index_ref[block + k : block + k + SUBLANES, cols])
                for k in (0, SUBLANES)
            ]
            permuted_ref[block : block + 16, cols] = jnp.concatenate(halves, axis=0).astype(jnp.bfloat16)
        chunk_copy(i).wait()
        new = []
        for c in range(columns):
            total = square[c]
            for r in range(0, LANES, 16):
                rows = pl.ds(pl.multiple_of(i * LANES + r, 16), 16)
                wide = genotypes_ref[rows, c * LANES : (c + 1) * LANES].astype(jnp.float32)
                wide = wide * wide
                total = total + (wide[:SUBLANES] + wide[SUBLANES:])
            new.append(total)
        return tuple(new)

    zero = jnp.zeros((SUBLANES, LANES), jnp.float32)
    square = lax.fori_loop(0, chunks, one_chunk, (zero,) * columns)
    for c in range(columns):
        out_ref[square_rows + c : square_rows + c + 1, :] = jnp.sum(square[c], axis=0, keepdims=True)

    source = source_rows(devices, block_rows, (perms, perms), 0)
    choice = (source == lax.broadcasted_iota(jnp.int32, (perms, perms), 1)).astype(jnp.bfloat16)
    ordered = jnp.dot(choice, permuted_ref[...], preferred_element_type=jnp.float32).astype(jnp.bfloat16)
    ones = jnp.ones((16, local_count), jnp.bfloat16)
    left = jnp.concatenate([ordered, ones], axis=0)
    width = 2 * LANES
    for first in range(0, variants, width):
        product = jnp.dot(left, genotypes_ref[:, first : first + width], preferred_element_type=jnp.float32)
        for c in range(first // LANES, (first + width) // LANES):
            part = product[:, c * LANES - first : (c + 1) * LANES - first]
            for r in range(0, perms, SUBLANES):
                out_ref[pl.ds(r * columns + c, SUBLANES, stride=columns), :] = part[r : r + SUBLANES]
            out_ref[perms * columns + c : perms * columns + c + 1, :] = part[perms : perms + 1]


def final_kernel(samples, sigma2_ref, mine_ref, got_ref, statistic_ref, largest_ref):
    block_rows, variants = statistic_ref.shape
    columns = variants // LANES
    kept = block_rows * columns
    count = mine_ref[2 * kept : 2 * kept + columns, :] + got_ref[kept : kept + columns, :]
    square = mine_ref[2 * kept + columns :, :] + got_ref[kept + columns :, :]
    spread = square - count * count / samples + 1.0
    scale = jnp.sqrt(sigma2_ref[0] * spread)
    for r in range(block_rows):
        rows = slice(r * columns, (r + 1) * columns)
        statistic = (mine_ref[rows, :] + got_ref[rows, :]) / scale
        for c in range(columns):
            statistic_ref[r : r + 1, c * LANES : (c + 1) * LANES] = statistic[c : c + 1]
        largest_ref[r] = jnp.max(jnp.abs(statistic))


def on_device(phenotype, perm_index, genotypes):
    devices = lax.axis_size("samp")
    samples = phenotype.shape[0]
    perms, local_count = perm_index.shape
    variants = genotypes.shape[1]
    columns = variants // LANES
    block_rows = perms // devices
    table_rows = samples // LANES
    vmem = pl.BlockSpec(memory_space=pltpu.VMEM)
    smem = pl.BlockSpec(memory_space=pltpu.SMEM)
    held, sigma2 = pl.pallas_call(
        functools.partial(partial_kernel, devices, block_rows),
        out_shape=(
            jax.ShapeDtypeStruct(((perms + 2) * columns, LANES), jnp.float32),
            jax.ShapeDtypeStruct((1,), jnp.float32),
        ),
        in_specs=[vmem, vmem, pl.BlockSpec(memory_space=pl.ANY)],
        out_specs=(vmem, smem),
        scratch_shapes=[
            pltpu.VMEM(genotypes.shape, jnp.bfloat16),
            pltpu.VMEM((table_rows // 2, LANES), jnp.int32),
            pltpu.VMEM(perm_index.shape, jnp.bfloat16),
            pltpu.SemaphoreType.DMA((local_count // LANES,)),
        ],
    )(phenotype.reshape(table_rows, LANES), perm_index, genotypes)

    even, odd = (round_bits(devices, side) for side in (False, True))
    kept = perms * columns
    for step in range(len(even)):
        pairs = [(i, i ^ (1 << (odd if i & 1 else even)[step])) for i in range(devices)]
        kept //= 2
        got = lax.ppermute(held[kept:], "samp", pairs)
        if step < len(even) - 1:
            held = jnp.concatenate([held[:kept] + got[:kept], held[2 * kept :] + got[kept:]], axis=0)

    statistic, largest = pl.pallas_call(
        functools.partial(final_kernel, samples),
        out_shape=(
            jax.ShapeDtypeStruct((block_rows, variants), jnp.float32),
            jax.ShapeDtypeStruct((block_rows,), jnp.float32),
        ),
        in_specs=[smem, vmem, vmem],
        out_specs=(vmem, smem),
    )(sigma2, held, got)
    if lax.axis_size("var") > 1:
        largest = lax.pmax(largest, "var")
    return statistic, largest


def solution(mesh):
    placed = (P(), P(None, "samp"), P("samp", "var"))
    return jax.shard_map(
        on_device,
        mesh=mesh,
        in_specs=placed,
        out_specs=(P("samp", "var"), P("samp")),
        check_vma=False,
    )
```

time: 192 us -> 42.1 us (0.22)
  waiting for transfers between devices: 85.1 us -> 10.1 us
  blocking collectives: 42 us -> 0 us
  matrix products: 25.9 us -> 0 us
  other arithmetic: 21 us -> 2.4 us
  Pallas kernels: 0 us -> 15.8 us
  between operations: 15.4 us -> 0.71 us
  starting transfers between devices: 0.04 us -> 11.2 us
    psum x1 -> x0, waiting for transfers between devices: 85.1 us -> none  [on_device(): scores, totals = lax.psum((partial_value, moments), 'samp')]
    psum x1 -> x0, blocking collectives: 42 us -> none  [on_device(): scores, totals = lax.psum((partial_value, moments), 'samp')]
    dot_general x10 -> x0, matrix products: 25.9 us -> none  [the longest x8 21.4 us: select_rows(): jnp.einsum('pnh,hc->pnc', upper_part, table, preferred_element_type=jnp.f...]
    pallas_call x0 -> x2, Pallas kernels: none -> 15.8 us  [the longest x1 13.7 us: on_device(): pl.pallas_call(functools.partial(partial_kernel, devices, block_rows), ou...]
    select_n x16 -> x0, other arithmetic: 12.5 us -> none  [the longest x8 6.3 us: select_rows(): index_rows // 128]
    ppermute x0 -> x5, starting transfers between devices: none -> 11.2 us  [on_device(): got = lax.ppermute(held[kept:], 'samp', pairs)]
    ppermute x0 -> x5, waiting for transfers between devices: none -> 10.1 us  [on_device(): got = lax.ppermute(held[kept:], 'samp', pairs)]
    dot_general x1 -> x0, other arithmetic: 3.22 us -> none  [on_device(): jnp.einsum('ij,ij->j', genotypes, genotypes, preferred_element_type=jnp.f...]
  transfers between devices with their start and end apart: 1 -> 5, of which waited for: 1 -> 5; matrix products, arithmetic and copies ran while one was open for 2% -> 1% of each run, Pallas kernels for 0% -> 0%
where the time goes in v1:
time: 42.1 us; the launch traced here: 41.8 us
  Pallas kernels  15.8 us (38%)
  starting transfers between devices  11.2 us (27%)
  waiting for transfers between devices  10.1 us (24%)
  other arithmetic  2.4 us (6%)
  local copies, waits for them, and re-layouts  1.58 us (4%)
  between operations  0.71 us (2%)
    pallas_call x1, Pallas kernels, on_device(): pl.pallas_call(functools.partial(partial_kernel, devices, block_rows), ou...  13.7 us
    ppermute x5, starting transfers between devices, on_device(): got = lax.ppermute(held[kept:], 'samp', pairs)  11.2 us
    ppermute x5, waiting for transfers between devices, on_device(): got = lax.ppermute(held[kept:], 'samp', pairs)  10.1 us
    pallas_call x1, Pallas kernels, on_device(): pl.pallas_call(functools.partial(final_kernel, samples), out_shape=(jax.S...  2.08 us
    add x4, other arithmetic, on_device(): held[:kept] + got[:kept]  1.02 us
    slice x1, local copies, waits for them, and re-layouts, on_device(): got = lax.ppermute(held[kept:], 'samp', pairs)  0.98 us
  transfers between devices with their start and end apart: 5, of which 5 were waited for; matrix products, arithmetic and copies ran while one was open for 1% of the time, Pallas kernels for 0%

profile of v1, /device:TPU:0, one launch (start us, length us, event | category | flops | bytes accessed | tf_op | source)
XLA Modules:
  0.0 41.8 jit_solution(13369469586737138909)
XLA Ops:
  0.6 13.7 %shard_map.50 = (f32[1056,128]{1,0:T(8,128)}, f32[1]{0:T(128)}) custom-call(f32[256,128]{1,0:T(8,128)} %bitcast.1, s32[64,1024]{1,0:T(8,128)} %index_ref.1, bf16[1024,2048]{1,0:T(8,128)(2,1)} %genotypes_hbm.1), custom_call_target="tpu_custom_call" | custom-call | tf_op jit(solution)/shard_map/pallas_call | solution.py:181
  14.4 1.0 %slice.55 = f32[544,128]{1,0:T(8,128)S(1)} slice(f32[1056,128]{1,0:T(8,128)} %get-tuple-element.5), slice={[512:1056], [0:128]} | slice | bytes 557056 | tf_op jit(solution)/shard_map/slice | solution.py:202
  15.4 0.6 %collective-permute-start = (f32[544,128]{1,0:T(8,128)S(1)}, f32[544,128]{1,0:T(8,128)S(1)}, u32[]{:S(2)}, u32[]{:S(2)}) collective-permute-start(f32[544,128]{1,0:T(8,128)S(1)} %slice.55), channel_id=1, source_target_pairs={{0,1},{1,0},{2,3},{3,2},{4,5},{5,4},{6,7},{7,6},{8,9},{9,8},{10,11... | collective-permute-start | bytes 835592 | tf_op jit(solution)/shard_map/ppermute | solution.py:202
  15.9 1.2 %collective-permute-done = f32[544,128]{1,0:T(8,128)S(1)} collective-permute-done((f32[544,128]{1,0:T(8,128)S(1)}, f32[544,128]{1,0:T(8,128)S(1)}, u32[]{:S(2)}, u32[]{:S(2)}) %collective-permute-start) | collective-permute-done | bytes 278560 | tf_op jit(solution)/shard_map/ppermute | solution.py:202
  17.1 0.7 %slice_add_fusion.7 = f32[32,128]{1,0:T(8,128)S(1)} fusion(f32[544,128]{1,0:T(8,128)S(1)} %collective-permute-done, f32[1056,128]{1,0:T(8,128)} %get-tuple-element.5), kind=kLoop, calls=%fused_computation.14 | loop fusion | flops 4096 | bytes 49152 | tf_op jit(solution)/shard_map/add | solution.py:204
  17.8 1.0 %slice_add_fusion = f32[512,128]{1,0:T(8,128)S(1)} fusion(f32[544,128]{1,0:T(8,128)S(1)} %collective-permute-done, f32[1056,128]{1,0:T(8,128)} %get-tuple-element.5), kind=kLoop, calls=%fused_computation | loop fusion | flops 65536 | bytes 786432 | tf_op jit(solution)/shard_map/add | solution.py:204
  18.8 2.9 %collective-permute-start.1 = (f32[288,128]{1,0:T(8,128)S(1)}, f32[288,128]{1,0:T(8,128)S(1)}, u32[]{:S(2)}, u32[]{:S(2)}) collective-permute-start(f32[288,128]{1,0:T(8,128)S(1)} %pad_maximum_fusion), channel_id=1, source_target_pairs={{0,2},{1,5},{2,0},{3,7},{4,6},{5,1},{6,4},{7,3},{8,10},{9,13},{10,... | collective-permute-start | bytes 442376 | tf_op jit(solution)/shard_map/ppermute | solution.py:202
  21.8 3.1 %collective-permute-done.1 = f32[288,128]{1,0:T(8,128)S(1)} collective-permute-done((f32[288,128]{1,0:T(8,128)S(1)}, f32[288,128]{1,0:T(8,128)S(1)}, u32[]{:S(2)}, u32[]{:S(2)}) %collective-permute-start.1) | collective-permute-done | bytes 147488 | tf_op jit(solution)/shard_map/ppermute | solution.py:202
  24.9 2.1 %collective-permute-start.2 = (f32[160,128]{1,0:T(8,128)S(1)}, f32[160,128]{1,0:T(8,128)S(1)}, u32[]{:S(2)}, u32[]{:S(2)}) collective-permute-start(f32[160,128]{1,0:T(8,128)S(1)} %pad_maximum_fusion.1), channel_id=1, source_target_pairs={{0,4},{1,3},{2,6},{3,1},{4,0},{5,7},{6,2},{7,5},{8,12},{9,11},{10,... | collective-permute-start | bytes 245768 | tf_op jit(solution)/shard_map/ppermute | solution.py:202
  27.0 2.4 %collective-permute-done.2 = f32[160,128]{1,0:T(8,128)S(1)} collective-permute-done((f32[160,128]{1,0:T(8,128)S(1)}, f32[160,128]{1,0:T(8,128)S(1)}, u32[]{:S(2)}, u32[]{:S(2)}) %collective-permute-start.2) | collective-permute-done | bytes 81952 | tf_op jit(solution)/shard_map/ppermute | solution.py:202
  29.5 2.1 %collective-permute-start.3 = (f32[96,128]{1,0:T(8,128)S(1)}, f32[96,128]{1,0:T(8,128)S(1)}, u32[]{:S(2)}, u32[]{:S(2)}) collective-permute-start(f32[96,128]{1,0:T(8,128)S(1)} %pad_maximum_fusion.3), channel_id=1, source_target_pairs={{0,8},{1,9},{2,10},{3,11},{4,12},{5,13},{6,14},{7,15},{8,0},{9,1},... | collective-permute-start | bytes 147464 | tf_op jit(solution)/shard_map/ppermute | solution.py:202
  31.6 2.1 %collective-permute-done.3 = f32[96,128]{1,0:T(8,128)S(1)} collective-permute-done((f32[96,128]{1,0:T(8,128)S(1)}, f32[96,128]{1,0:T(8,128)S(1)}, u32[]{:S(2)}, u32[]{:S(2)}) %collective-permute-start.3) | collective-permute-done | bytes 49184 | tf_op jit(solution)/shard_map/ppermute | solution.py:202
  33.7 3.4 %collective-permute-start.4 = (f32[64,128]{1,0:T(8,128)S(1)}, f32[64,128]{1,0:T(8,128)S(1)}, u32[]{:S(2)}, u32[]{:S(2)}) collective-permute-start(f32[64,128]{1,0:T(8,128)S(1)} %fusion), channel_id=1, source_target_pairs={{0,16},{1,17},{2,18},{3,19},{4,20},{5,21},{6,22},{7,23},{8,24},{9,... | collective-permute-start | bytes 98312 | tf_op jit(solution)/shard_map/ppermute | solution.py:202
  37.2 0.6 %pad_maximum_fusion.2.mine_ref = f32[96,128]{1,0:T(8,128)} fusion(f32[32,128]{1,0:T(8,128)S(1)} %slice_add_fusion.4, f32[64,128]{1,0:T(8,128)S(1)} %slice_add_fusion.3), kind=kLoop, calls=%fused_computation.6 | loop fusion | flops 12288 | bytes 98304 | tf_op jit(solution)/shard_map/concatenate | solution.py:204
  37.8 1.3 %collective-permute-done.4.got_ref = f32[64,128]{1,0:T(8,128)S(1)} collective-permute-done((f32[64,128]{1,0:T(8,128)S(1)}, f32[64,128]{1,0:T(8,128)S(1)}, u32[]{:S(2)}, u32[]{:S(2)}) %collective-permute-start.4) | collective-permute-done | bytes 32800 | tf_op jit(solution)/shard_map/ppermute | solution.py:202
  39.1 0.0 copy-start
  39.1 0.6 %copy-done = f32[64,128]{1,0:T(8,128)} copy-done((f32[64,128]{1,0:T(8,128)}, f32[64,128]{1,0:T(8,128)S(1)}, u32[]{:S(2)}) %copy-start) | copy-done | bytes 32792
  39.7 2.1 %shard_map.51 = (f32[2,2048]{1,0:T(2,128)}, f32[2]{0:T(128)}) custom-call(f32[1]{0:T(128)} %get-tuple-element.4.sigma2_ref, f32[96,128]{1,0:T(8,128)} %pad_maximum_fusion.2.mine_ref, f32[64,128]{1,0:T(8,128)} %copy-done), custom_call_target="tpu_custom_call" | custom-call | tf_op jit(solution)/shard_map/pallas_call | solution.py:206
  (10 shorter events, 0.1 us)
Async XLA Ops:
  15.4 1.7 %collective-permute-start = (f32[544,128]{1,0:T(8,128)S(1)}, f32[544,128]{1,0:T(8,128)S(1)}, u32[]{:S(2)}, u32[]{:S(2)}) collective-permute-start(f32[544,128]{1,0:T(8,128)S(1)} %slice.55), channel_id=1, source_target_pairs={{0,1},{1,0},{2,3},{3,2},{4,5},{5,4},{6,7},{7,6},{8,9},{9,8},{10,11... | collective-permute-start | bytes 835592 | tf_op jit(solution)/shard_map/ppermute | solution.py:202
  18.8 6.0 %collective-permute-start.1 = (f32[288,128]{1,0:T(8,128)S(1)}, f32[288,128]{1,0:T(8,128)S(1)}, u32[]{:S(2)}, u32[]{:S(2)}) collective-permute-start(f32[288,128]{1,0:T(8,128)S(1)} %pad_maximum_fusion), channel_id=1, source_target_pairs={{0,2},{1,5},{2,0},{3,7},{4,6},{5,1},{6,4},{7,3},{8,10},{9,13},{10,... | collective-permute-start | bytes 442376 | tf_op jit(solution)/shard_map/ppermute | solution.py:202
  24.9 4.5 %collective-permute-start.2 = (f32[160,128]{1,0:T(8,128)S(1)}, f32[160,128]{1,0:T(8,128)S(1)}, u32[]{:S(2)}, u32[]{:S(2)}) collective-permute-start(f32[160,128]{1,0:T(8,128)S(1)} %pad_maximum_fusion.1), channel_id=1, source_target_pairs={{0,4},{1,3},{2,6},{3,1},{4,0},{5,7},{6,2},{7,5},{8,12},{9,11},{10,... | collective-permute-start | bytes 245768 | tf_op jit(solution)/shard_map/ppermute | solution.py:202
  29.5 4.2 %collective-permute-start.3 = (f32[96,128]{1,0:T(8,128)S(1)}, f32[96,128]{1,0:T(8,128)S(1)}, u32[]{:S(2)}, u32[]{:S(2)}) collective-permute-start(f32[96,128]{1,0:T(8,128)S(1)} %pad_maximum_fusion.3), channel_id=1, source_target_pairs={{0,8},{1,9},{2,10},{3,11},{4,12},{5,13},{6,14},{7,15},{8,0},{9,1},... | collective-permute-start | bytes 147464 | tf_op jit(solution)/shard_map/ppermute | solution.py:202
  33.7 5.3 %collective-permute-start.4 = (f32[64,128]{1,0:T(8,128)S(1)}, f32[64,128]{1,0:T(8,128)S(1)}, u32[]{:S(2)}, u32[]{:S(2)}) collective-permute-start(f32[64,128]{1,0:T(8,128)S(1)} %fusion), channel_id=1, source_target_pairs={{0,16},{1,17},{2,18},{3,19},{4,20},{5,21},{6,22},{7,23},{8,24},{9,... | collective-permute-start | bytes 98312 | tf_op jit(solution)/shard_map/ppermute | solution.py:202
  39.1 0.6 %copy-start = (f32[64,128]{1,0:T(8,128)}, f32[64,128]{1,0:T(8,128)S(1)}, u32[]{:S(2)}) copy-start(f32[64,128]{1,0:T(8,128)S(1)} %collective-permute-done.4.got_ref) | copy-start | bytes 98308

commit v2 on v1

--- a/solution.py
+++ b/solution.py
@@ -88,7 +88,7 @@
     return owner * block_rows + inner
 
 
-def partial_kernel(devices, block_rows, phenotype_ref, index_ref, genotypes_hbm, out_ref, sigma2_ref,
+def partial_kernel(devices, block_rows, phenotype_ref, index_ref, genotypes_hbm, kept_ref, sent_ref, sigma2_ref,
                    genotypes_ref, table_ref, permuted_ref, semaphores):
     perms, local_count = index_ref.shape
     variants = genotypes_ref.shape[1]
@@ -110,7 +110,9 @@
     words = table_ref.shape[0]
     table_ref[...] = code[:words] | (code[words:] << 16)
 
-    square_rows = (perms + 1) * columns
+    half = perms // 2
+    count_row = half * columns
+    square_row = count_row + columns
 
     def one_chunk(i, square):
         cols = pl.ds(pl.multiple_of(i * LANES, LANES), LANES)
@@ -135,7 +137,7 @@
     zero = jnp.zeros((SUBLANES, LANES), jnp.float32)
     square = lax.fori_loop(0, chunks, one_chunk, (zero,) * columns)
     for c in range(columns):
-        out_ref[square_rows + c : square_rows + c + 1, :] = jnp.sum(square[c], axis=0, keepdims=True)
+        sent_ref[square_row + c : square_row + c + 1, :] = jnp.sum(square[c], axis=0, keepdims=True)
 
     source = source_rows(devices, block_rows, (perms, perms), 0)
     choice = (source == lax.broadcasted_iota(jnp.int32, (perms, perms), 1)).astype(jnp.bfloat16)
@@ -147,22 +149,24 @@
         product = jnp.dot(left, genotypes_ref[:, first : first + width], preferred_element_type=jnp.float32)
         for c in range(first // LANES, (first + width) // LANES):
             part = product[:, c * LANES - first : (c + 1) * LANES - first]
-            for r in range(0, perms, SUBLANES):
-                out_ref[pl.ds(r * columns + c, SUBLANES, stride=columns), :] = part[r : r + SUBLANES]
-            out_ref[perms * columns + c : perms * columns + c + 1, :] = part[perms : perms + 1]
-
-
-def final_kernel(samples, sigma2_ref, mine_ref, got_ref, statistic_ref, largest_ref):
+            for r in range(0, half, SUBLANES):
+                rows = pl.ds(r * columns + c, SUBLANES, stride=columns)
+                kept_ref[rows, :] = part[r : r + SUBLANES]
+                sent_ref[rows, :] = part[half + r : half + r + SUBLANES]
+            sent_ref[count_row + c : count_row + c + 1, :] = part[perms : perms + 1]
+
+
+def final_kernel(samples, sigma2_ref, held_ref, moments_ref, got_ref, statistic_ref, largest_ref):
     block_rows, variants = statistic_ref.shape
     columns = variants // LANES
     kept = block_rows * columns
-    count = mine_ref[2 * kept : 2 * kept + columns, :] + got_ref[kept : kept + columns, :]
-    square = mine_ref[2 * kept + columns :, :] + got_ref[kept + columns :, :]
+    count = moments_ref[:columns, :] + got_ref[kept : kept + columns, :]
+    square = moments_ref[columns:, :] + got_ref[kept + columns :, :]
     spread = square - count * count / samples + 1.0
     scale = jnp.sqrt(sigma2_ref[0] * spread)
     for r in range(block_rows):
         rows = slice(r * columns, (r + 1) * columns)
-        statistic = (mine_ref[rows, :] + got_ref[rows, :]) / scale
+        statistic = (held_ref[rows, :] + got_ref[rows, :]) / scale
         for c in range(columns):
             statistic_ref[r : r + 1, c * LANES : (c + 1) * LANES] = statistic[c : c + 1]
         largest_ref[r] = jnp.max(jnp.abs(statistic))
@@ -178,30 +182,36 @@
     table_rows = samples // LANES
     vmem = pl.BlockSpec(memory_space=pltpu.VMEM)
     smem = pl.BlockSpec(memory_space=pltpu.SMEM)
-    held, sigma2 = pl.pallas_call(
+    kept = perms // 2 * columns
+    held, sent, sigma2 = pl.pallas_call(
         functools.partial(partial_kernel, devices, block_rows),
         out_shape=(
-            jax.ShapeDtypeStruct(((perms + 2) * columns, LANES), jnp.float32),
+            jax.ShapeDtypeStruct((kept, LANES), jnp.float32),
+            jax.ShapeDtypeStruct((kept + 2 * columns, LANES), jnp.float32),
             jax.ShapeDtypeStruct((1,), jnp.float32),
         ),
         in_specs=[vmem, vmem, pl.BlockSpec(memory_space=pl.ANY)],
-        out_specs=(vmem, smem),
+        out_specs=(vmem, vmem, smem),
         scratch_shapes=[
             pltpu.VMEM(genotypes.shape, jnp.bfloat16),
             pltpu.VMEM((table_rows // 2, LANES), jnp.int32),
             pltpu.VMEM(perm_index.shape, jnp.bfloat16),
             pltpu.SemaphoreType.DMA((local_count // LANES,)),
         ],
+        compiler_params=pltpu.CompilerParams(vmem_limit_bytes=51 << 20),
     )(phenotype.reshape(table_rows, LANES), perm_index, genotypes)
 
     even, odd = (round_bits(devices, side) for side in (False, True))
-    kept = perms * columns
+    moments = sent[kept:]
     for step in range(len(even)):
         pairs = [(i, i ^ (1 << (odd if i & 1 else even)[step])) for i in range(devices)]
-        kept //= 2
-        got = lax.ppermute(held[kept:], "samp", pairs)
+        got = lax.ppermute(sent, "samp", pairs)
         if step < len(even) - 1:
-            held = jnp.concatenate([held[:kept] + got[:kept], held[2 * kept :] + got[kept:]], axis=0)
+            scores = held + got[:kept]
+            moments = moments + got[kept:]
+            kept //= 2
+            held = scores[:kept]
+            sent = jnp.concatenate([scores[kept:], moments], axis=0)
 
     statistic, largest = pl.pallas_call(
         functools.partial(final_kernel, samples),
@@ -209,9 +219,10 @@
             jax.ShapeDtypeStruct((block_rows, variants), jnp.float32),
             jax.ShapeDtypeStruct((block_rows,), jnp.float32),
         ),
-        in_specs=[smem, vmem, vmem],
+        in_specs=[smem, vmem, vmem, vmem],
         out_specs=(vmem, smem),
-    )(sigma2, held, got)
+        compiler_params=pltpu.CompilerParams(vmem_limit_bytes=2 << 20),
+    )(sigma2, held, moments, got)
     if lax.axis_size("var") > 1:
         largest = lax.pmax(largest, "var")
     return statistic, largest

time: 42.1 us -> 38 us (0.903)
  Pallas kernels: 15.8 us -> 13.3 us
  other arithmetic: 2.4 us -> 0.12 us
  waiting for transfers between devices: 10.1 us -> 10.7 us
    pallas_call x1, Pallas kernels: 13.7 us -> 11.9 us  [on_device(): pl.pallas_call(functools.partial(partial_kernel, devices, block_rows), ou...]
    add x8 -> x7, other arithmetic: 1.76 us -> 0.08 us  [the longest x4 0.06 us: on_device(): scores = held + got[:kept]]
    unnamed x2 -> x4, local copies, waits for them, and re-layouts: 0.61 us -> 1.85 us
    slice x1 -> x3, local copies, waits for them, and re-layouts: 0.98 us -> 0.02 us  [on_device(): sent = jnp.concatenate([scores[kept:], moments], axis=0)]
    pallas_call x1, Pallas kernels: 2.08 us -> 1.34 us  [on_device(): pl.pallas_call(functools.partial(final_kernel, samples), out_shape=(jax.S...]
    ppermute x5, waiting for transfers between devices: 10.1 us -> 10.7 us  [on_device(): got = lax.ppermute(sent, 'samp', pairs)]
    concatenate x5 -> x4, other arithmetic: 0.65 us -> 0.03 us  [on_device(): sent = jnp.concatenate([scores[kept:], moments], axis=0)]
  transfers between devices with their start and end apart: 5 -> 5, of which waited for: 5 -> 5; matrix products, arithmetic and copies ran while one was open for 1% -> 0% of each run, Pallas kernels for 0% -> 0%
where the time goes in v2:
time: 38 us; the launch traced here: 37.9 us
  Pallas kernels  13.3 us (35%)
  starting transfers between devices  11.2 us (29%)
  waiting for transfers between devices  10.7 us (28%)
  local copies, waits for them, and re-layouts  1.87 us (5%)
  between operations  0.74 us (2%)
    pallas_call x1, Pallas kernels, on_device(): pl.pallas_call(functools.partial(partial_kernel, devices, block_rows), ou...  11.9 us
    ppermute x5, starting transfers between devices, on_device(): got = lax.ppermute(sent, 'samp', pairs)  11.2 us
    ppermute x5, waiting for transfers between devices, on_device(): got = lax.ppermute(sent, 'samp', pairs)  10.7 us
    unnamed x4, local copies, waits for them, and re-layouts  1.85 us
    pallas_call x1, Pallas kernels, on_device(): pl.pallas_call(functools.partial(final_kernel, samples), out_shape=(jax.S...  1.34 us
  transfers between devices with their start and end apart: 5, of which 5 were waited for; matrix products, arithmetic and copies ran while one was open for 0% of the time, Pallas kernels for 0%

profile of v2, /device:TPU:0, one launch (start us, length us, event | category | flops | bytes accessed | tf_op | source)
XLA Modules:
  0.0 37.9 jit_solution(7070807783252767170)
XLA Ops:
  0.6 0.0 copy-start
  0.6 0.9 %copy-done = s32[64,1024]{1,0:T(8,128)S(1)} copy-done((s32[64,1024]{1,0:T(8,128)S(1)}, s32[64,1024]{1,0:T(8,128)}, u32[]{:S(2)}) %copy-start) | copy-done | bytes 262168
  1.6 0.0 copy-start.1
  1.6 0.9 %copy-done.1 = f32[32768]{0:T(1024)S(1)} copy-done((f32[32768]{0:T(1024)S(1)}, f32[32768]{0:T(1024)}, u32[]{:S(2)}) %copy-start.1) | copy-done | bytes 131096
  2.5 11.9 %shard_map.50 = (f32[512,128]{1,0:T(8,128)S(1)}, f32[544,128]{1,0:T(8,128)S(1)}, f32[1]{0:T(128)}) custom-call(f32[256,128]{1,0:T(8,128)S(1)} %bitcast.1, s32[64,1024]{1,0:T(8,128)S(1)} %copy-done, bf16[1024,2048]{1,0:T(8,128)(2,1)} %genotypes_hbm.1), custom_call_target="tpu_custom_call" | custom-call | tf_op jit(solution)/shard_map/pallas_call | solution.py:186
  14.4 0.6 %collective-permute-start = (f32[544,128]{1,0:T(8,128)S(1)}, f32[544,128]{1,0:T(8,128)S(1)}, u32[]{:S(2)}, u32[]{:S(2)}) collective-permute-start(f32[544,128]{1,0:T(8,128)S(1)} %get-tuple-element.7), channel_id=1, source_target_pairs={{0,1},{1,0},{2,3},{3,2},{4,5},{5,4},{6,7},{7,6},{8,9},{9,8},{10,11... | collective-permute-start | bytes 835592 | tf_op jit(solution)/shard_map/ppermute | solution.py:208
  15.0 1.2 %collective-permute-done = f32[544,128]{1,0:T(8,128)S(1)} collective-permute-done((f32[544,128]{1,0:T(8,128)S(1)}, f32[544,128]{1,0:T(8,128)S(1)}, u32[]{:S(2)}, u32[]{:S(2)}) %collective-permute-start) | collective-permute-done | bytes 278560 | tf_op jit(solution)/shard_map/ppermute | solution.py:208
  16.3 2.9 %collective-permute-start.1 = (f32[288,128]{1,0:T(8,128)S(1)}, f32[288,128]{1,0:T(8,128)S(1)}, u32[]{:S(2)}, u32[]{:S(2)}) collective-permute-start(f32[288,128]{1,0:T(8,128)S(1)} %pad_maximum_fusion), channel_id=1, source_target_pairs={{0,2},{1,5},{2,0},{3,7},{4,6},{5,1},{6,4},{7,3},{8,10},{9,13},{10,... | collective-permute-start | bytes 442376 | tf_op jit(solution)/shard_map/ppermute | solution.py:208
  19.2 3.1 %collective-permute-done.1 = f32[288,128]{1,0:T(8,128)S(1)} collective-permute-done((f32[288,128]{1,0:T(8,128)S(1)}, f32[288,128]{1,0:T(8,128)S(1)}, u32[]{:S(2)}, u32[]{:S(2)}) %collective-permute-start.1) | collective-permute-done | bytes 147488 | tf_op jit(solution)/shard_map/ppermute | solution.py:208
  22.4 2.1 %collective-permute-start.2 = (f32[160,128]{1,0:T(8,128)S(1)}, f32[160,128]{1,0:T(8,128)S(1)}, u32[]{:S(2)}, u32[]{:S(2)}) collective-permute-start(f32[160,128]{1,0:T(8,128)S(1)} %pad_maximum_fusion.1), channel_id=1, source_target_pairs={{0,4},{1,3},{2,6},{3,1},{4,0},{5,7},{6,2},{7,5},{8,12},{9,11},{10,... | collective-permute-start | bytes 245768 | tf_op jit(solution)/shard_map/ppermute | solution.py:208
  24.5 2.4 %collective-permute-done.2 = f32[160,128]{1,0:T(8,128)S(1)} collective-permute-done((f32[160,128]{1,0:T(8,128)S(1)}, f32[160,128]{1,0:T(8,128)S(1)}, u32[]{:S(2)}, u32[]{:S(2)}) %collective-permute-start.2) | collective-permute-done | bytes 81952 | tf_op jit(solution)/shard_map/ppermute | solution.py:208
  26.9 2.1 %collective-permute-start.3 = (f32[96,128]{1,0:T(8,128)S(1)}, f32[96,128]{1,0:T(8,128)S(1)}, u32[]{:S(2)}, u32[]{:S(2)}) collective-permute-start(f32[96,128]{1,0:T(8,128)S(1)} %pad_maximum_fusion.2), channel_id=1, source_target_pairs={{0,8},{1,9},{2,10},{3,11},{4,12},{5,13},{6,14},{7,15},{8,0},{9,1},... | collective-permute-start | bytes 147464 | tf_op jit(solution)/shard_map/ppermute | solution.py:208
  29.1 2.1 %collective-permute-done.3 = f32[96,128]{1,0:T(8,128)S(1)} collective-permute-done((f32[96,128]{1,0:T(8,128)S(1)}, f32[96,128]{1,0:T(8,128)S(1)}, u32[]{:S(2)}, u32[]{:S(2)}) %collective-permute-start.3) | collective-permute-done | bytes 49184 | tf_op jit(solution)/shard_map/ppermute | solution.py:208
  31.2 3.4 %collective-permute-start.4 = (f32[64,128]{1,0:T(8,128)S(1)}, f32[64,128]{1,0:T(8,128)S(1)}, u32[]{:S(2)}, u32[]{:S(2)}) collective-permute-start(f32[64,128]{1,0:T(8,128)S(1)} %pad_maximum_fusion.3), channel_id=1, source_target_pairs={{0,16},{1,17},{2,18},{3,19},{4,20},{5,21},{6,22},{7,23},{8,24},{9,... | collective-permute-start | bytes 98312 | tf_op jit(solution)/shard_map/ppermute | solution.py:208
  34.6 1.9 %collective-permute-done.4.got_ref = f32[64,128]{1,0:T(8,128)S(1)} collective-permute-done((f32[64,128]{1,0:T(8,128)S(1)}, f32[64,128]{1,0:T(8,128)S(1)}, u32[]{:S(2)}, u32[]{:S(2)}) %collective-permute-start.4) | collective-permute-done | bytes 32800 | tf_op jit(solution)/shard_map/ppermute | solution.py:208
  36.5 1.3 %shard_map.51 = (f32[2,2048]{1,0:T(2,128)}, f32[2]{0:T(128)}) custom-call(f32[1]{0:T(128)} %get-tuple-element.5.sigma2_ref, f32[32,128]{1,0:T(8,128)S(1)} %get-tuple-element.9.held_ref, f32[32,128]{1,0:T(8,128)S(1)} %get-tuple-element.10.moments_ref, f32[64,128]{1,0:T(8,128)S(1)} %collective-permute-done.4.got_ref), custom_call_target="tpu_custom_call" | custom-call | tf_op jit(solution)/shard_map/pallas_call | solution.py:216
  (15 shorter events, 0.1 us)
Async XLA Ops:
  0.6 1.0 %copy-start = (s32[64,1024]{1,0:T(8,128)S(1)}, s32[64,1024]{1,0:T(8,128)}, u32[]{:S(2)}) copy-start(s32[64,1024]{1,0:T(8,128)} %index_ref.1) | copy-start | bytes 786436
  1.6 0.9 %copy-start.1 = (f32[32768]{0:T(1024)S(1)}, f32[32768]{0:T(1024)}, u32[]{:S(2)}) copy-start(f32[32768]{0:T(1024)} %param.3) | copy-start | bytes 393220
  14.4 1.7 %collective-permute-start = (f32[544,128]{1,0:T(8,128)S(1)}, f32[544,128]{1,0:T(8,128)S(1)}, u32[]{:S(2)}, u32[]{:S(2)}) collective-permute-start(f32[544,128]{1,0:T(8,128)S(1)} %get-tuple-element.7), channel_id=1, source_target_pairs={{0,1},{1,0},{2,3},{3,2},{4,5},{5,4},{6,7},{7,6},{8,9},{9,8},{10,11... | collective-permute-start | bytes 835592 | tf_op jit(solution)/shard_map/ppermute | solution.py:208
  16.3 6.0 %collective-permute-start.1 = (f32[288,128]{1,0:T(8,128)S(1)}, f32[288,128]{1,0:T(8,128)S(1)}, u32[]{:S(2)}, u32[]{:S(2)}) collective-permute-start(f32[288,128]{1,0:T(8,128)S(1)} %pad_maximum_fusion), channel_id=1, source_target_pairs={{0,2},{1,5},{2,0},{3,7},{4,6},{5,1},{6,4},{7,3},{8,10},{9,13},{10,... | collective-permute-start | bytes 442376 | tf_op jit(solution)/shard_map/ppermute | solution.py:208
  22.4 4.5 %collective-permute-start.2 = (f32[160,128]{1,0:T(8,128)S(1)}, f32[160,128]{1,0:T(8,128)S(1)}, u32[]{:S(2)}, u32[]{:S(2)}) collective-permute-start(f32[160,128]{1,0:T(8,128)S(1)} %pad_maximum_fusion.1), channel_id=1, source_target_pairs={{0,4},{1,3},{2,6},{3,1},{4,0},{5,7},{6,2},{7,5},{8,12},{9,11},{10,... | collective-permute-start | bytes 245768 | tf_op jit(solution)/shard_map/ppermute | solution.py:208
  26.9 4.2 %collective-permute-start.3 = (f32[96,128]{1,0:T(8,128)S(1)}, f32[96,128]{1,0:T(8,128)S(1)}, u32[]{:S(2)}, u32[]{:S(2)}) collective-permute-start(f32[96,128]{1,0:T(8,128)S(1)} %pad_maximum_fusion.2), channel_id=1, source_target_pairs={{0,8},{1,9},{2,10},{3,11},{4,12},{5,13},{6,14},{7,15},{8,0},{9,1},... | collective-permute-start | bytes 147464 | tf_op jit(solution)/shard_map/ppermute | solution.py:208
  31.2 5.3 %collective-permute-start.4 = (f32[64,128]{1,0:T(8,128)S(1)}, f32[64,128]{1,0:T(8,128)S(1)}, u32[]{:S(2)}, u32[]{:S(2)}) collective-permute-start(f32[64,128]{1,0:T(8,128)S(1)} %pad_maximum_fusion.3), channel_id=1, source_target_pairs={{0,16},{1,17},{2,18},{3,19},{4,20},{5,21},{6,22},{7,23},{8,24},{9,... | collective-permute-start | bytes 98312 | tf_op jit(solution)/shard_map/ppermute | solution.py:208

commit v3 on v2

--- a/solution.py
+++ b/solution.py
@@ -9,6 +9,8 @@
 
 LANES = 128
 SUBLANES = 8
+RANK = jnp.bfloat16
+PRODUCT_BLOCKS = (1,4,6)
 
 LANE_GATHER = lax.GatherDimensionNumbers(
     offset_dims=(),
@@ -69,6 +71,44 @@
     return decode(code)
 
 
+def look_up_by_product(table_ref, rank_ref, index_ref, first, cols):
+    one, zero = jnp.ones((), jnp.bfloat16), jnp.zeros((), jnp.bfloat16)
+    depth = table_ref.shape[1]
+    sublane = lax.broadcasted_iota(jnp.int32, (SUBLANES, LANES), 0)
+    picked = []
+    for pair in range(0, SUBLANES, 2):
+        index = [
+            jnp.broadcast_to(index_ref[first + pair + k : first + pair + k + 1, cols], (SUBLANES, LANES))
+            for k in (0, 1)
+        ]
+        hot = []
+        for k in (0, 1):
+            high = (index[k] >> 7).astype(jnp.float32)
+            high = jnp.concatenate([high, high], axis=0).astype(RANK)
+            hot.append(
+                jnp.concatenate(
+                    [jnp.where(high == rank_ref[r : r + 16, :], one, zero) for r in range(0, depth, 16)], axis=0
+                )
+            )
+        found = jnp.dot(table_ref[...], jnp.concatenate(hot, axis=1), preferred_element_type=jnp.float32)
+        for k in (0, 1):
+            lanes = index[k] & (LANES - 1)
+            level = [
+                found[r : r + SUBLANES, k * LANES : (k + 1) * LANES] for r in range(0, LANES, SUBLANES)
+            ]
+            bit = SUBLANES
+            while len(level) > 1:
+                mask = (lanes & bit) != 0
+                level = [jnp.where(mask, level[j + 1], level[j]) for j in range(0, len(level), 2)]
+                bit *= 2
+            picked.append(jnp.where((lanes & (SUBLANES - 1)) == sublane, level[0], 0.0))
+    spread = jnp.concatenate(picked, axis=0).astype(jnp.bfloat16)
+    row = lax.broadcasted_iota(jnp.int32, (SUBLANES, SUBLANES * SUBLANES), 0)
+    column = lax.broadcasted_iota(jnp.int32, (SUBLANES, SUBLANES * SUBLANES), 1)
+    gather_rows = (column // SUBLANES == row).astype(jnp.bfloat16)
+    return jnp.dot(gather_rows, spread, preferred_element_type=jnp.float32)
+
+
 def source_rows(devices, block_rows, shape, axis):
     me = lax.axis_index("samp")
     row = lax.broadcasted_iota(jnp.int32, shape, axis)
@@ -88,50 +128,71 @@
     return owner * block_rows + inner
 
 
-def partial_kernel(devices, block_rows, phenotype_ref, index_ref, genotypes_hbm, kept_ref, sent_ref, sigma2_ref,
-                   genotypes_ref, table_ref, permuted_ref, semaphores):
+def partial_kernel(devices, block_rows, phenotype_hbm, index_hbm, genotypes_hbm, kept_ref, sent_ref, sigma2_ref,
+                   phenotype_ref, index_ref, genotypes_ref, table_ref, turned_ref, rank_ref, permuted_ref, semaphores):
     perms, local_count = index_ref.shape
     variants = genotypes_ref.shape[1]
     columns = variants // LANES
     chunks = local_count // LANES
-    samples = phenotype_ref.shape[0] * LANES
+    table_rows = phenotype_ref.shape[0]
+    samples = table_rows * LANES
+    words = table_ref.shape[0]
 
     def chunk_copy(i):
         rows = pl.ds(pl.multiple_of(i * LANES, LANES), LANES)
         return pltpu.make_async_copy(genotypes_hbm.at[rows], genotypes_ref.at[rows], semaphores.at[i])
 
+    phenotype_copy = pltpu.make_async_copy(phenotype_hbm, phenotype_ref, semaphores.at[chunks])
+    index_copy = pltpu.make_async_copy(index_hbm, index_ref, semaphores.at[chunks + 1])
+    phenotype_copy.start()
+    index_copy.start()
     for i in range(chunks):
         chunk_copy(i).start()
 
-    phenotype = phenotype_ref[...]
-    centred = phenotype - jnp.sum(phenotype) / samples
-    sigma2_ref[0] = jnp.sum(centred * centred) / samples + 1e-05
-    code = encode(centred.astype(jnp.bfloat16).astype(jnp.float32))
-    words = table_ref.shape[0]
-    table_ref[...] = code[:words] | (code[words:] << 16)
-
+    for r in range(0, table_rows, 16):
+        rank = lax.broadcasted_iota(jnp.int32, (16, LANES), 0) + r
+        rank_ref[r : r + 16, :] = rank.astype(jnp.float32).astype(RANK)
+    phenotype_copy.wait()
+    mean = jnp.sum(phenotype_ref[...]) / samples
+    total = jnp.zeros((SUBLANES, LANES), jnp.float32)
+    for r in range(0, words, SUBLANES):
+        codes = []
+        for first in (r, r + words):
+            centred = phenotype_ref[first : first + SUBLANES, :] - mean
+            total = total + centred * centred
+            rounded = centred.astype(jnp.bfloat16).astype(jnp.float32)
+            phenotype_ref[first : first + SUBLANES, :] = rounded
+            codes.append(encode(rounded))
+        table_ref[r : r + SUBLANES, :] = codes[0] | (codes[1] << 16)
+    sigma2_ref[0] = jnp.sum(total) / samples + 1e-05
+    for r in range(0, table_rows, LANES):
+        turned_ref[:, r : r + LANES] = phenotype_ref[r : r + LANES, :].T.astype(jnp.bfloat16)
+
+    index_copy.wait()
     half = perms // 2
     count_row = half * columns
     square_row = count_row + columns
 
     def one_chunk(i, square):
         cols = pl.ds(pl.multiple_of(i * LANES, LANES), LANES)
-        for block in range(0, perms, 16):
-            halves = [
-                look_up(table_ref, index_ref[block + k : block + k + SUBLANES, cols])
-                for k in (0, SUBLANES)
-            ]
-            permuted_ref[block : block + 16, cols] = jnp.concatenate(halves, axis=0).astype(jnp.bfloat16)
         chunk_copy(i).wait()
+        blocks = perms // SUBLANES
         new = []
-        for c in range(columns):
-            total = square[c]
-            for r in range(0, LANES, 16):
-                rows = pl.ds(pl.multiple_of(i * LANES + r, 16), 16)
-                wide = genotypes_ref[rows, c * LANES : (c + 1) * LANES].astype(jnp.float32)
-                wide = wide * wide
-                total = total + (wide[:SUBLANES] + wide[SUBLANES:])
-            new.append(total)
+        for block in range(blocks):
+            first = block * SUBLANES
+            if block in PRODUCT_BLOCKS:
+                value = look_up_by_product(turned_ref, rank_ref, index_ref, first, cols)
+            else:
+                value = look_up(table_ref, index_ref[first : first + SUBLANES, cols])
+            permuted_ref[first : first + SUBLANES, cols] = value
+            for c in range(block * columns // blocks, (block + 1) * columns // blocks):
+                total = square[c]
+                for r in range(0, LANES, 16):
+                    rows = pl.ds(pl.multiple_of(i * LANES + r, 16), 16)
+                    wide = genotypes_ref[rows, c * LANES : (c + 1) * LANES].astype(jnp.float32)
+                    wide = wide * wide
+                    total = total + (wide[:SUBLANES] + wide[SUBLANES:])
+                new.append(total)
         return tuple(new)
 
     zero = jnp.zeros((SUBLANES, LANES), jnp.float32)
@@ -141,7 +202,7 @@
 
     source = source_rows(devices, block_rows, (perms, perms), 0)
     choice = (source == lax.broadcasted_iota(jnp.int32, (perms, perms), 1)).astype(jnp.bfloat16)
-    ordered = jnp.dot(choice, permuted_ref[...], preferred_element_type=jnp.float32).astype(jnp.bfloat16)
+    ordered = jnp.dot(choice, permuted_ref[...].astype(jnp.bfloat16), preferred_element_type=jnp.float32).astype(jnp.bfloat16)
     ones = jnp.ones((16, local_count), jnp.bfloat16)
     left = jnp.concatenate([ordered, ones], axis=0)
     width = 2 * LANES
@@ -182,6 +243,10 @@
     table_rows = samples // LANES
     vmem = pl.BlockSpec(memory_space=pltpu.VMEM)
     smem = pl.BlockSpec(memory_space=pltpu.SMEM)
+    inputs = [
+        pltpu.with_memory_space_constraint(array, pltpu.HBM)
+        for array in (phenotype.reshape(table_rows, LANES), perm_index, genotypes)
+    ]
     kept = perms // 2 * columns
     held, sent, sigma2 = pl.pallas_call(
         functools.partial(partial_kernel, devices, block_rows),
@@ -190,16 +255,20 @@
             jax.ShapeDtypeStruct((kept + 2 * columns, LANES), jnp.float32),
             jax.ShapeDtypeStruct((1,), jnp.float32),
         ),
-        in_specs=[vmem, vmem, pl.BlockSpec(memory_space=pl.ANY)],
+        in_specs=[pl.BlockSpec(memory_space=pltpu.HBM)] * 3,
         out_specs=(vmem, vmem, smem),
         scratch_shapes=[
+            pltpu.VMEM((table_rows, LANES), jnp.float32),
+            pltpu.VMEM(perm_index.shape, jnp.int32),
             pltpu.VMEM(genotypes.shape, jnp.bfloat16),
             pltpu.VMEM((table_rows // 2, LANES), jnp.int32),
-            pltpu.VMEM(perm_index.shape, jnp.bfloat16),
-            pltpu.SemaphoreType.DMA((local_count // LANES,)),
+            pltpu.VMEM((LANES, table_rows), jnp.bfloat16),
+            pltpu.VMEM((table_rows, LANES), RANK),
+            pltpu.VMEM(perm_index.shape, jnp.float32),
+            pltpu.SemaphoreType.DMA((local_count // LANES + 2,)),
         ],
-        compiler_params=pltpu.CompilerParams(vmem_limit_bytes=51 << 20),
-    )(phenotype.reshape(table_rows, LANES), perm_index, genotypes)
+        compiler_params=pltpu.CompilerParams(vmem_limit_bytes=16 << 20),
+    )(*inputs)
 
     even, odd = (round_bits(devices, side) for side in (False, True))
     moments = sent[kept:]

time: 38 us -> 34.2 us (0.900)
  Pallas kernels: 13.3 us -> 11.3 us
  local copies, waits for them, and re-layouts: 1.87 us -> 0.02 us
    pallas_call x1, Pallas kernels: 11.9 us -> 9.93 us  [on_device(): pl.pallas_call(functools.partial(partial_kernel, devices, block_rows), ou...]
    unnamed x4 -> x0, local copies, waits for them, and re-layouts: 1.85 us -> none
where the time goes in v3:
time: 34.2 us; the launch traced here: 34 us
  Pallas kernels  11.3 us (33%)
  starting transfers between devices  11.2 us (33%)
  waiting for transfers between devices  10.7 us (31%)
  between operations  0.73 us (2%)
    ppermute x5, starting transfers between devices, on_device(): got = lax.ppermute(sent, 'samp', pairs)  11.2 us
    ppermute x5, waiting for transfers between devices, on_device(): got = lax.ppermute(sent, 'samp', pairs)  10.7 us
    pallas_call x1, Pallas kernels, on_device(): pl.pallas_call(functools.partial(partial_kernel, devices, block_rows), ou...  9.93 us
    pallas_call x1, Pallas kernels, on_device(): pl.pallas_call(functools.partial(final_kernel, samples), out_shape=(jax.S...  1.35 us
  transfers between devices with their start and end apart: 5, of which 5 were waited for; matrix products, arithmetic and copies ran while one was open for 0% of the time, Pallas kernels for 0%

profile of v3, /device:TPU:0, one launch (start us, length us, event | category | flops | bytes accessed | tf_op | source)
XLA Modules:
  0.0 34.0 jit_solution(1485316265911906384)
XLA Ops:
  0.6 9.9 %shard_map.50 = (f32[512,128]{1,0:T(8,128)S(1)}, f32[544,128]{1,0:T(8,128)S(1)}, f32[1]{0:T(128)}) custom-call(f32[256,128]{1,0:T(8,128)} %bitcast.1, s32[64,1024]{1,0:T(8,128)} %index_hbm.1, bf16[1024,2048]{1,0:T(8,128)(2,1)} %genotypes_hbm.1), custom_call_target="tpu_custom_call" | custom-call | tf_op jit(solution)/shard_map/pallas_call | solution.py:251
  10.6 0.6 %collective-permute-start = (f32[544,128]{1,0:T(8,128)S(1)}, f32[544,128]{1,0:T(8,128)S(1)}, u32[]{:S(2)}, u32[]{:S(2)}) collective-permute-start(f32[544,128]{1,0:T(8,128)S(1)} %get-tuple-element.7), channel_id=1, source_target_pairs={{0,1},{1,0},{2,3},{3,2},{4,5},{5,4},{6,7},{7,6},{8,9},{9,8},{10,11... | collective-permute-start | bytes 835592 | tf_op jit(solution)/shard_map/ppermute | solution.py:277
  11.1 1.2 %collective-permute-done = f32[544,128]{1,0:T(8,128)S(1)} collective-permute-done((f32[544,128]{1,0:T(8,128)S(1)}, f32[544,128]{1,0:T(8,128)S(1)}, u32[]{:S(2)}, u32[]{:S(2)}) %collective-permute-start) | collective-permute-done | bytes 278560 | tf_op jit(solution)/shard_map/ppermute | solution.py:277
  12.4 2.9 %collective-permute-start.1 = (f32[288,128]{1,0:T(8,128)S(1)}, f32[288,128]{1,0:T(8,128)S(1)}, u32[]{:S(2)}, u32[]{:S(2)}) collective-permute-start(f32[288,128]{1,0:T(8,128)S(1)} %pad_maximum_fusion), channel_id=1, source_target_pairs={{0,2},{1,5},{2,0},{3,7},{4,6},{5,1},{6,4},{7,3},{8,10},{9,13},{10,... | collective-permute-start | bytes 442376 | tf_op jit(solution)/shard_map/ppermute | solution.py:277
  15.3 3.1 %collective-permute-done.1 = f32[288,128]{1,0:T(8,128)S(1)} collective-permute-done((f32[288,128]{1,0:T(8,128)S(1)}, f32[288,128]{1,0:T(8,128)S(1)}, u32[]{:S(2)}, u32[]{:S(2)}) %collective-permute-start.1) | collective-permute-done | bytes 147488 | tf_op jit(solution)/shard_map/ppermute | solution.py:277
  18.5 2.1 %collective-permute-start.2 = (f32[160,128]{1,0:T(8,128)S(1)}, f32[160,128]{1,0:T(8,128)S(1)}, u32[]{:S(2)}, u32[]{:S(2)}) collective-permute-start(f32[160,128]{1,0:T(8,128)S(1)} %pad_maximum_fusion.1), channel_id=1, source_target_pairs={{0,4},{1,3},{2,6},{3,1},{4,0},{5,7},{6,2},{7,5},{8,12},{9,11},{10,... | collective-permute-start | bytes 245768 | tf_op jit(solution)/shard_map/ppermute | solution.py:277
  20.6 2.4 %collective-permute-done.2 = f32[160,128]{1,0:T(8,128)S(1)} collective-permute-done((f32[160,128]{1,0:T(8,128)S(1)}, f32[160,128]{1,0:T(8,128)S(1)}, u32[]{:S(2)}, u32[]{:S(2)}) %collective-permute-start.2) | collective-permute-done | bytes 81952 | tf_op jit(solution)/shard_map/ppermute | solution.py:277
  23.1 2.1 %collective-permute-start.3 = (f32[96,128]{1,0:T(8,128)S(1)}, f32[96,128]{1,0:T(8,128)S(1)}, u32[]{:S(2)}, u32[]{:S(2)}) collective-permute-start(f32[96,128]{1,0:T(8,128)S(1)} %pad_maximum_fusion.2), channel_id=1, source_target_pairs={{0,8},{1,9},{2,10},{3,11},{4,12},{5,13},{6,14},{7,15},{8,0},{9,1},... | collective-permute-start | bytes 147464 | tf_op jit(solution)/shard_map/ppermute | solution.py:277
  25.2 2.1 %collective-permute-done.3 = f32[96,128]{1,0:T(8,128)S(1)} collective-permute-done((f32[96,128]{1,0:T(8,128)S(1)}, f32[96,128]{1,0:T(8,128)S(1)}, u32[]{:S(2)}, u32[]{:S(2)}) %collective-permute-start.3) | collective-permute-done | bytes 49184 | tf_op jit(solution)/shard_map/ppermute | solution.py:277
  27.3 3.4 %collective-permute-start.4 = (f32[64,128]{1,0:T(8,128)S(1)}, f32[64,128]{1,0:T(8,128)S(1)}, u32[]{:S(2)}, u32[]{:S(2)}) collective-permute-start(f32[64,128]{1,0:T(8,128)S(1)} %pad_maximum_fusion.3), channel_id=1, source_target_pairs={{0,16},{1,17},{2,18},{3,19},{4,20},{5,21},{6,22},{7,23},{8,24},{9,... | collective-permute-start | bytes 98312 | tf_op jit(solution)/shard_map/ppermute | solution.py:277
  30.8 1.9 %collective-permute-done.4.got_ref = f32[64,128]{1,0:T(8,128)S(1)} collective-permute-done((f32[64,128]{1,0:T(8,128)S(1)}, f32[64,128]{1,0:T(8,128)S(1)}, u32[]{:S(2)}, u32[]{:S(2)}) %collective-permute-start.4) | collective-permute-done | bytes 32800 | tf_op jit(solution)/shard_map/ppermute | solution.py:277
  32.7 1.3 %shard_map.51 = (f32[2,2048]{1,0:T(2,128)}, f32[2]{0:T(128)}) custom-call(f32[1]{0:T(128)} %get-tuple-element.5.sigma2_ref, f32[32,128]{1,0:T(8,128)S(1)} %get-tuple-element.9.held_ref, f32[32,128]{1,0:T(8,128)S(1)} %get-tuple-element.10.moments_ref, f32[64,128]{1,0:T(8,128)S(1)} %collective-permute-done.4.got_ref), custom_call_target="tpu_custom_call" | custom-call | tf_op jit(solution)/shard_map/pallas_call | solution.py:285
  (15 shorter events, 0.1 us)
Async XLA Ops:
  10.6 1.8 %collective-permute-start = (f32[544,128]{1,0:T(8,128)S(1)}, f32[544,128]{1,0:T(8,128)S(1)}, u32[]{:S(2)}, u32[]{:S(2)}) collective-permute-start(f32[544,128]{1,0:T(8,128)S(1)} %get-tuple-element.7), channel_id=1, source_target_pairs={{0,1},{1,0},{2,3},{3,2},{4,5},{5,4},{6,7},{7,6},{8,9},{9,8},{10,11... | collective-permute-start | bytes 835592 | tf_op jit(solution)/shard_map/ppermute | solution.py:277
  12.4 6.0 %collective-permute-start.1 = (f32[288,128]{1,0:T(8,128)S(1)}, f32[288,128]{1,0:T(8,128)S(1)}, u32[]{:S(2)}, u32[]{:S(2)}) collective-permute-start(f32[288,128]{1,0:T(8,128)S(1)} %pad_maximum_fusion), channel_id=1, source_target_pairs={{0,2},{1,5},{2,0},{3,7},{4,6},{5,1},{6,4},{7,3},{8,10},{9,13},{10,... | collective-permute-start | bytes 442376 | tf_op jit(solution)/shard_map/ppermute | solution.py:277
  18.5 4.5 %collective-permute-start.2 = (f32[160,128]{1,0:T(8,128)S(1)}, f32[160,128]{1,0:T(8,128)S(1)}, u32[]{:S(2)}, u32[]{:S(2)}) collective-permute-start(f32[160,128]{1,0:T(8,128)S(1)} %pad_maximum_fusion.1), channel_id=1, source_target_pairs={{0,4},{1,3},{2,6},{3,1},{4,0},{5,7},{6,2},{7,5},{8,12},{9,11},{10,... | collective-permute-start | bytes 245768 | tf_op jit(solution)/shard_map/ppermute | solution.py:277
  23.1 4.2 %collective-permute-start.3 = (f32[96,128]{1,0:T(8,128)S(1)}, f32[96,128]{1,0:T(8,128)S(1)}, u32[]{:S(2)}, u32[]{:S(2)}) collective-permute-start(f32[96,128]{1,0:T(8,128)S(1)} %pad_maximum_fusion.2), channel_id=1, source_target_pairs={{0,8},{1,9},{2,10},{3,11},{4,12},{5,13},{6,14},{7,15},{8,0},{9,1},... | collective-permute-start | bytes 147464 | tf_op jit(solution)/shard_map/ppermute | solution.py:277
  27.3 5.3 %collective-permute-start.4 = (f32[64,128]{1,0:T(8,128)S(1)}, f32[64,128]{1,0:T(8,128)S(1)}, u32[]{:S(2)}, u32[]{:S(2)}) collective-permute-start(f32[64,128]{1,0:T(8,128)S(1)} %pad_maximum_fusion.3), channel_id=1, source_target_pairs={{0,16},{1,17},{2,18},{3,19},{4,20},{5,21},{6,22},{7,23},{8,24},{9,... | collective-permute-start | bytes 98312 | tf_op jit(solution)/shard_map/ppermute | solution.py:277

commit v4 on v3

--- a/solution.py
+++ b/solution.py
@@ -10,7 +10,8 @@
 LANES = 128
 SUBLANES = 8
 RANK = jnp.bfloat16
-PRODUCT_BLOCKS = (1,4,6)
+PRODUCT_BLOCKS = (1, 4, 6)
+WIDTHS = (1, 2, 2)
 
 LANE_GATHER = lax.GatherDimensionNumbers(
     offset_dims=(),
@@ -26,6 +27,15 @@
     if odd_core and len(bits) >= 2:
         bits[0], bits[1] = bits[1], bits[0]
     return [0] + bits
+
+
+def round_widths(devices):
+    bits = devices.bit_length() - 1
+    widths = []
+    for width in WIDTHS:
+        if sum(widths) + width <= bits:
+            widths.append(width)
+    return widths + [1] * (bits - sum(widths))
 
 
 def encode(value):
@@ -217,17 +227,18 @@
             sent_ref[count_row + c : count_row + c + 1, :] = part[perms : perms + 1]
 
 
-def final_kernel(samples, sigma2_ref, held_ref, moments_ref, got_ref, statistic_ref, largest_ref):
+def final_kernel(samples, sigma2_ref, held_ref, moments_ref, *refs):
+    *got_refs, statistic_ref, largest_ref = refs
     block_rows, variants = statistic_ref.shape
     columns = variants // LANES
     kept = block_rows * columns
-    count = moments_ref[:columns, :] + got_ref[kept : kept + columns, :]
-    square = moments_ref[columns:, :] + got_ref[kept + columns :, :]
+    count = sum((got_ref[kept : kept + columns, :] for got_ref in got_refs), moments_ref[:columns, :])
+    square = sum((got_ref[kept + columns :, :] for got_ref in got_refs), moments_ref[columns:, :])
     spread = square - count * count / samples + 1.0
     scale = jnp.sqrt(sigma2_ref[0] * spread)
     for r in range(block_rows):
         rows = slice(r * columns, (r + 1) * columns)
-        statistic = (held_ref[rows, :] + got_ref[rows, :]) / scale
+        statistic = sum((got_ref[rows, :] for got_ref in got_refs), held_ref[rows, :]) / scale
         for c in range(columns):
             statistic_ref[r : r + 1, c * LANES : (c + 1) * LANES] = statistic[c : c + 1]
         largest_ref[r] = jnp.max(jnp.abs(statistic))
@@ -272,15 +283,28 @@
 
     even, odd = (round_bits(devices, side) for side in (False, True))
     moments = sent[kept:]
-    for step in range(len(even)):
-        pairs = [(i, i ^ (1 << (odd if i & 1 else even)[step])) for i in range(devices)]
-        got = lax.ppermute(sent, "samp", pairs)
-        if step < len(even) - 1:
-            scores = held + got[:kept]
-            moments = moments + got[kept:]
-            kept //= 2
+    messages = [sent]
+    widths = round_widths(devices)
+    done = 0
+    for step, width in enumerate(widths):
+        got = []
+        for part, message in enumerate(messages, 1):
+            flips = [
+                sum(1 << bits[done + k] for k in range(width) if (part >> (width - 1 - k)) & 1) for bits in (even, odd)
+            ]
+            pairs = [(i, i ^ flips[i & 1]) for i in range(devices)]
+            got.append(lax.ppermute(message, "samp", pairs))
+        done += width
+        if done < len(even):
+            scores = sum((g[:kept] for g in got), held)
+            moments = sum((g[kept:] for g in got), moments)
+            following = widths[step + 1]
+            kept >>= following
             held = scores[:kept]
-            sent = jnp.concatenate([scores[kept:], moments], axis=0)
+            messages = [
+                jnp.concatenate([scores[part * kept : (part + 1) * kept], moments], axis=0)
+                for part in range(1, 1 << following)
+            ]
 
     statistic, largest = pl.pallas_call(
         functools.partial(final_kernel, samples),
@@ -288,10 +312,10 @@
             jax.ShapeDtypeStruct((block_rows, variants), jnp.float32),
             jax.ShapeDtypeStruct((block_rows,), jnp.float32),
         ),
-        in_specs=[smem, vmem, vmem, vmem],
+        in_specs=[smem] + [vmem] * (2 + len(got)),
         out_specs=(vmem, smem),
         compiler_params=pltpu.CompilerParams(vmem_limit_bytes=2 << 20),
-    )(sigma2, held, moments, got)
+    )(sigma2, held, moments, *got)
     if lax.axis_size("var") > 1:
         largest = lax.pmax(largest, "var")
     return statistic, largest

time: 34.2 us -> 32.2 us (0.942)
  starting transfers between devices: 11.2 us -> 9.5 us
    ppermute x5 -> x7, starting transfers between devices: 11.2 us -> 9.5 us  [on_device(): got.append(lax.ppermute(message, 'samp', pairs))]
    ppermute x5 -> x7, waiting for transfers between devices: 10.7 us -> 10.5 us  [on_device(): got.append(lax.ppermute(message, 'samp', pairs))]
  transfers between devices with their start and end apart: 5 -> 7, of which waited for: 5 -> 7; matrix products, arithmetic and copies ran while one was open for 0% -> 0% of each run, Pallas kernels for 0% -> 0%
where the time goes in v4:
time: 32.2 us; the launch traced here: 32 us
  Pallas kernels  11.2 us (35%)
  waiting for transfers between devices  10.5 us (33%)
  starting transfers between devices  9.5 us (30%)
  between operations  0.69 us (2%)
    ppermute x7, waiting for transfers between devices, on_device(): got.append(lax.ppermute(message, 'samp', pairs))  10.5 us
    pallas_call x1, Pallas kernels, on_device(): pl.pallas_call(functools.partial(partial_kernel, devices, block_rows), ou...  9.93 us
    ppermute x7, starting transfers between devices, on_device(): got.append(lax.ppermute(message, 'samp', pairs))  9.5 us
    pallas_call x1, Pallas kernels, on_device(): pl.pallas_call(functools.partial(final_kernel, samples), out_shape=(jax.S...  1.28 us
  transfers between devices with their start and end apart: 7, of which 7 were waited for; matrix products, arithmetic and copies ran while one was open for 0% of the time, Pallas kernels for 0%

profile of v4, /device:TPU:0, one launch (start us, length us, event | category | flops | bytes accessed | tf_op | source)
XLA Modules:
  0.0 32.0 jit_solution(7935786357006397368)
XLA Ops:
  0.6 9.9 %shard_map.50 = (f32[512,128]{1,0:T(8,128)S(1)}, f32[544,128]{1,0:T(8,128)S(1)}, f32[1]{0:T(128)}) custom-call(f32[256,128]{1,0:T(8,128)} %bitcast.1, s32[64,1024]{1,0:T(8,128)} %index_hbm.1, bf16[1024,2048]{1,0:T(8,128)(2,1)} %genotypes_hbm.1), custom_call_target="tpu_custom_call" | custom-call | tf_op jit(solution)/shard_map/pallas_call | solution.py:262
  10.6 0.6 %collective-permute-start = (f32[544,128]{1,0:T(8,128)S(1)}, f32[544,128]{1,0:T(8,128)S(1)}, u32[]{:S(2)}, u32[]{:S(2)}) collective-permute-start(f32[544,128]{1,0:T(8,128)S(1)} %get-tuple-element.7), channel_id=1, source_target_pairs={{0,1},{1,0},{2,3},{3,2},{4,5},{5,4},{6,7},{7,6},{8,9},{9,8},{10,11... | collective-permute-start | bytes 835592 | tf_op jit(solution)/shard_map/ppermute | solution.py:296
  11.1 1.2 %collective-permute-done = f32[544,128]{1,0:T(8,128)S(1)} collective-permute-done((f32[544,128]{1,0:T(8,128)S(1)}, f32[544,128]{1,0:T(8,128)S(1)}, u32[]{:S(2)}, u32[]{:S(2)}) %collective-permute-start) | collective-permute-done | bytes 278560 | tf_op jit(solution)/shard_map/ppermute | solution.py:296
  12.4 2.9 %collective-permute-start.1 = (f32[160,128]{1,0:T(8,128)S(1)}, f32[160,128]{1,0:T(8,128)S(1)}, u32[]{:S(2)}, u32[]{:S(2)}) collective-permute-start(f32[160,128]{1,0:T(8,128)S(1)} %get-tuple-element.18), channel_id=1, source_target_pairs={{0,4},{1,3},{2,6},{3,1},{4,0},{5,7},{6,2},{7,5},{8,12},{9,11},{10,... | collective-permute-start | bytes 245768 | tf_op jit(solution)/shard_map/ppermute | solution.py:296
  15.4 1.5 %collective-permute-start.2 = (f32[160,128]{1,0:T(8,128)S(1)}, f32[160,128]{1,0:T(8,128)S(1)}, u32[]{:S(2)}, u32[]{:S(2)}) collective-permute-start(f32[160,128]{1,0:T(8,128)S(1)} %get-tuple-element.19), channel_id=1, source_target_pairs={{0,2},{1,5},{2,0},{3,7},{4,6},{5,1},{6,4},{7,3},{8,10},{9,13},{10,... | collective-permute-start | bytes 245768 | tf_op jit(solution)/shard_map/ppermute | solution.py:296
  16.9 0.1 collective-permute-start.3
  16.9 0.9 %collective-permute-done.1 = f32[160,128]{1,0:T(8,128)S(1)} collective-permute-done((f32[160,128]{1,0:T(8,128)S(1)}, f32[160,128]{1,0:T(8,128)S(1)}, u32[]{:S(2)}, u32[]{:S(2)}) %collective-permute-start.1) | collective-permute-done | bytes 81952 | tf_op jit(solution)/shard_map/ppermute | solution.py:296
  17.8 2.8 %collective-permute-done.2 = f32[160,128]{1,0:T(8,128)S(1)} collective-permute-done((f32[160,128]{1,0:T(8,128)S(1)}, f32[160,128]{1,0:T(8,128)S(1)}, u32[]{:S(2)}, u32[]{:S(2)}) %collective-permute-start.2) | collective-permute-done | bytes 81952 | tf_op jit(solution)/shard_map/ppermute | solution.py:296
  20.6 1.6 %collective-permute-done.3 = f32[160,128]{1,0:T(8,128)S(1)} collective-permute-done((f32[160,128]{1,0:T(8,128)S(1)}, f32[160,128]{1,0:T(8,128)S(1)}, u32[]{:S(2)}, u32[]{:S(2)}) %collective-permute-start.3) | collective-permute-done | bytes 81952 | tf_op jit(solution)/shard_map/ppermute | solution.py:296
  22.3 3.7 %collective-permute-start.6 = (f32[64,128]{1,0:T(8,128)S(1)}, f32[64,128]{1,0:T(8,128)S(1)}, u32[]{:S(2)}, u32[]{:S(2)}) collective-permute-start(f32[64,128]{1,0:T(8,128)S(1)} %get-tuple-element.15), channel_id=1, source_target_pairs={{0,24},{1,25},{2,26},{3,27},{4,28},{5,29},{6,30},{7,31},{8,16},{9,... | collective-permute-start | bytes 98312 | tf_op jit(solution)/shard_map/ppermute | solution.py:296
  25.9 0.0 collective-permute-start.5
  25.9 0.8 %collective-permute-start.4 = (f32[64,128]{1,0:T(8,128)S(1)}, f32[64,128]{1,0:T(8,128)S(1)}, u32[]{:S(2)}, u32[]{:S(2)}) collective-permute-start(f32[64,128]{1,0:T(8,128)S(1)} %get-tuple-element.17), channel_id=1, source_target_pairs={{0,16},{1,17},{2,18},{3,19},{4,20},{5,21},{6,22},{7,23},{8,24},{9,... | collective-permute-start | bytes 98312 | tf_op jit(solution)/shard_map/ppermute | solution.py:296
  26.7 1.4 %collective-permute-done.6.refs_2_ = f32[64,128]{1,0:T(8,128)S(1)} collective-permute-done((f32[64,128]{1,0:T(8,128)S(1)}, f32[64,128]{1,0:T(8,128)S(1)}, u32[]{:S(2)}, u32[]{:S(2)}) %collective-permute-start.6) | collective-permute-done | bytes 32800 | tf_op jit(solution)/shard_map/ppermute | solution.py:296
  28.1 1.7 %collective-permute-done.5.refs_1_ = f32[64,128]{1,0:T(8,128)S(1)} collective-permute-done((f32[64,128]{1,0:T(8,128)S(1)}, f32[64,128]{1,0:T(8,128)S(1)}, u32[]{:S(2)}, u32[]{:S(2)}) %collective-permute-start.5) | collective-permute-done | bytes 32800 | tf_op jit(solution)/shard_map/ppermute | solution.py:296
  29.8 0.9 %collective-permute-done.4.refs_0_ = f32[64,128]{1,0:T(8,128)S(1)} collective-permute-done((f32[64,128]{1,0:T(8,128)S(1)}, f32[64,128]{1,0:T(8,128)S(1)}, u32[]{:S(2)}, u32[]{:S(2)}) %collective-permute-start.4) | collective-permute-done | bytes 32800 | tf_op jit(solution)/shard_map/ppermute | solution.py:296
  30.7 1.3 %shard_map.51 = (f32[2,2048]{1,0:T(2,128)}, f32[2]{0:T(128)}) custom-call(f32[1]{0:T(128)} %get-tuple-element.5.sigma2_ref, f32[32,128]{1,0:T(8,128)S(1)} %get-tuple-element.14.held_ref, f32[32,128]{1,0:T(8,128)S(1)} %get-tuple-element.21.moments_ref, f32[64,128]{1,0:T(8,128)S(1)} %collective-permute-done.4.refs_0_, ...), custom_call_target="tpu_custom_call" | custom-call | tf_op jit(solution)/shard_map/pallas_call | solution.py:309
  (7 shorter events, 0.1 us)
Async XLA Ops:
  10.6 1.8 %collective-permute-start = (f32[544,128]{1,0:T(8,128)S(1)}, f32[544,128]{1,0:T(8,128)S(1)}, u32[]{:S(2)}, u32[]{:S(2)}) collective-permute-start(f32[544,128]{1,0:T(8,128)S(1)} %get-tuple-element.7), channel_id=1, source_target_pairs={{0,1},{1,0},{2,3},{3,2},{4,5},{5,4},{6,7},{7,6},{8,9},{9,8},{10,11... | collective-permute-start | bytes 835592 | tf_op jit(solution)/shard_map/ppermute | solution.py:296
  12.4 5.4 %collective-permute-start.1 = (f32[160,128]{1,0:T(8,128)S(1)}, f32[160,128]{1,0:T(8,128)S(1)}, u32[]{:S(2)}, u32[]{:S(2)}) collective-permute-start(f32[160,128]{1,0:T(8,128)S(1)} %get-tuple-element.18), channel_id=1, source_target_pairs={{0,4},{1,3},{2,6},{3,1},{4,0},{5,7},{6,2},{7,5},{8,12},{9,11},{10,... | collective-permute-start | bytes 245768 | tf_op jit(solution)/shard_map/ppermute | solution.py:296
  15.4 5.3 %collective-permute-start.2 = (f32[160,128]{1,0:T(8,128)S(1)}, f32[160,128]{1,0:T(8,128)S(1)}, u32[]{:S(2)}, u32[]{:S(2)}) collective-permute-start(f32[160,128]{1,0:T(8,128)S(1)} %get-tuple-element.19), channel_id=1, source_target_pairs={{0,2},{1,5},{2,0},{3,7},{4,6},{5,1},{6,4},{7,3},{8,10},{9,13},{10,... | collective-permute-start | bytes 245768 | tf_op jit(solution)/shard_map/ppermute | solution.py:296
  16.9 5.3 %collective-permute-start.3 = (f32[160,128]{1,0:T(8,128)S(1)}, f32[160,128]{1,0:T(8,128)S(1)}, u32[]{:S(2)}, u32[]{:S(2)}) collective-permute-start(f32[160,128]{1,0:T(8,128)S(1)} %get-tuple-element.20), channel_id=1, source_target_pairs={{0,6},{1,7},{2,4},{3,5},{4,2},{5,3},{6,0},{7,1},{8,14},{9,15},{10,... | collective-permute-start | bytes 245768 | tf_op jit(solution)/shard_map/ppermute | solution.py:296
  22.3 5.9 %collective-permute-start.6 = (f32[64,128]{1,0:T(8,128)S(1)}, f32[64,128]{1,0:T(8,128)S(1)}, u32[]{:S(2)}, u32[]{:S(2)}) collective-permute-start(f32[64,128]{1,0:T(8,128)S(1)} %get-tuple-element.15), channel_id=1, source_target_pairs={{0,24},{1,25},{2,26},{3,27},{4,28},{5,29},{6,30},{7,31},{8,16},{9,... | collective-permute-start | bytes 98312 | tf_op jit(solution)/shard_map/ppermute | solution.py:296
  25.9 3.9 %collective-permute-start.5 = (f32[64,128]{1,0:T(8,128)S(1)}, f32[64,128]{1,0:T(8,128)S(1)}, u32[]{:S(2)}, u32[]{:S(2)}) collective-permute-start(f32[64,128]{1,0:T(8,128)S(1)} %get-tuple-element.16), channel_id=1, source_target_pairs={{0,8},{1,9},{2,10},{3,11},{4,12},{5,13},{6,14},{7,15},{8,0},{9,1},... | collective-permute-start | bytes 98312 | tf_op jit(solution)/shard_map/ppermute | solution.py:296
  25.9 4.8 %collective-permute-start.4 = (f32[64,128]{1,0:T(8,128)S(1)}, f32[64,128]{1,0:T(8,128)S(1)}, u32[]{:S(2)}, u32[]{:S(2)}) collective-permute-start(f32[64,128]{1,0:T(8,128)S(1)} %get-tuple-element.17), channel_id=1, source_target_pairs={{0,16},{1,17},{2,18},{3,19},{4,20},{5,21},{6,22},{7,23},{8,24},{9,... | collective-permute-start | bytes 98312 | tf_op jit(solution)/shard_map/ppermute | solution.py:296

commit v5 on v4

--- a/solution.py
+++ b/solution.py
@@ -10,7 +10,7 @@
 LANES = 128
 SUBLANES = 8
 RANK = jnp.bfloat16
-PRODUCT_BLOCKS = (1, 4, 6)
+PAIR = 2
 WIDTHS = (1, 2, 2)
 
 LANE_GATHER = lax.GatherDimensionNumbers(
@@ -119,34 +119,69 @@
     return jnp.dot(gather_rows, spread, preferred_element_type=jnp.float32)
 
 
-def source_rows(devices, block_rows, shape, axis):
+def owner_masks(devices, odd_core):
+    rounds = devices.bit_length() - 1
+    bits = round_bits(devices, odd_core)
+    return [
+        sum(((slot >> (rounds - 1 - k)) & 1) << bit for k, bit in enumerate(bits)) for slot in range(devices)
+    ]
+
+
+def order_rows(devices, block_rows, index_ref, ordered_ref):
     me = lax.axis_index("samp")
-    row = lax.broadcasted_iota(jnp.int32, shape, axis)
-    slot, inner = row // block_rows, row % block_rows
-    rounds = devices.bit_length() - 1
-    even, odd = (round_bits(devices, side) for side in (False, True))
-
-    def spread(bits):
-        owner = jnp.zeros(shape, jnp.int32)
-        for k, bit in enumerate(bits):
-            owner = owner | (((slot >> (rounds - 1 - k)) & 1) << bit)
-        return owner
-
-    upper = (slot >> (rounds - 1)) & 1
-    use_odd = ((me & 1) ^ upper) == 1
-    owner = me ^ jnp.where(use_odd, spread(odd), spread(even))
-    return owner * block_rows + inner
-
-
-def partial_kernel(devices, block_rows, phenotype_hbm, index_hbm, genotypes_hbm, kept_ref, sent_ref, sigma2_ref,
-                   phenotype_ref, index_ref, genotypes_ref, table_ref, turned_ref, rank_ref, permuted_ref, semaphores):
-    perms, local_count = index_ref.shape
+    even, odd = (owner_masks(devices, side) for side in (False, True))
+    for slot in range(devices):
+        side = (me & 1) ^ (1 if slot >= devices // 2 else 0)
+        row = (me ^ jnp.where(side == 1, odd[slot], even[slot])) * block_rows
+        for r in range(block_rows):
+            place = slot * block_rows + r
+            ordered_ref[place : place + 1, :] = index_ref[pl.ds(row + r, 1), :]
+
+
+def fill_ranks(rank_ref):
+    for r in range(0, rank_ref.shape[0], 16):
+        rank = lax.broadcasted_iota(jnp.int32, (16, LANES), 0) + r
+        rank_ref[r : r + 16, :] = rank.astype(jnp.float32).astype(RANK)
+
+
+def look_up_pair(table_ref, turned_ref, rank_ref, index_ref, permuted_ref, first_row, i):
+    blocks = permuted_ref.shape[0] // SUBLANES
+    for u in range(PAIR):
+        cols = pl.ds(pl.multiple_of((i * PAIR + u) * LANES, LANES), LANES)
+        for block in range(blocks):
+            first = first_row + block * SUBLANES
+            if ((u * blocks + block) * 3) % 8 < 3:
+                value = look_up_by_product(turned_ref, rank_ref, index_ref, first, cols)
+            else:
+                value = look_up(table_ref, index_ref[first : first + SUBLANES, cols])
+            permuted_ref[block * SUBLANES : (block + 1) * SUBLANES, cols] = value
+        yield u
+
+
+def multiply(left, rows, genotypes_ref, out_ref):
     variants = genotypes_ref.shape[1]
     columns = variants // LANES
+    width = 2 * LANES
+    for first in range(0, variants, width):
+        product = jnp.dot(left, genotypes_ref[:, first : first + width], preferred_element_type=jnp.float32)
+        for c in range(first // LANES, (first + width) // LANES):
+            part = product[:, c * LANES - first : (c + 1) * LANES - first]
+            for r in range(0, rows, SUBLANES):
+                out_ref[pl.ds(r * columns + c, SUBLANES, stride=columns), :] = part[r : r + SUBLANES]
+            if left.shape[0] > rows:
+                out_ref[rows * columns + c : rows * columns + c + 1, :] = part[rows : rows + 1]
+
+
+def head_kernel(devices, block_rows, phenotype_hbm, index_hbm, genotypes_hbm, sent_ref, genotypes_ref, ordered_ref,
+                table_ref, turned_ref, sigma2_ref, phenotype_ref, index_ref, rank_ref, permuted_ref, square_ref,
+                semaphores):
+    perms, local_count = index_ref.shape
+    columns = genotypes_ref.shape[1] // LANES
     chunks = local_count // LANES
     table_rows = phenotype_ref.shape[0]
     samples = table_rows * LANES
     words = table_ref.shape[0]
+    half = perms // 2
 
     def chunk_copy(i):
         rows = pl.ds(pl.multiple_of(i * LANES, LANES), LANES)
@@ -159,9 +194,8 @@
     for i in range(chunks):
         chunk_copy(i).start()
 
-    for r in range(0, table_rows, 16):
-        rank = lax.broadcasted_iota(jnp.int32, (16, LANES), 0) + r
-        rank_ref[r : r + 16, :] = rank.astype(jnp.float32).astype(RANK)
+    fill_ranks(rank_ref)
+    square_ref[...] = jnp.zeros_like(square_ref)
     phenotype_copy.wait()
     mean = jnp.sum(phenotype_ref[...]) / samples
     total = jnp.zeros((SUBLANES, LANES), jnp.float32)
@@ -174,57 +208,48 @@
             phenotype_ref[first : first + SUBLANES, :] = rounded
             codes.append(encode(rounded))
         table_ref[r : r + SUBLANES, :] = codes[0] | (codes[1] << 16)
-    sigma2_ref[0] = jnp.sum(total) / samples + 1e-05
+    sigma2_ref[...] = jnp.full(sigma2_ref.shape, jnp.sum(total) / samples + 1e-05)
     for r in range(0, table_rows, LANES):
         turned_ref[:, r : r + LANES] = phenotype_ref[r : r + LANES, :].T.astype(jnp.bfloat16)
 
     index_copy.wait()
-    half = perms // 2
-    count_row = half * columns
-    square_row = count_row + columns
-
-    def one_chunk(i, square):
-        cols = pl.ds(pl.multiple_of(i * LANES, LANES), LANES)
-        chunk_copy(i).wait()
-        blocks = perms // SUBLANES
-        new = []
-        for block in range(blocks):
-            first = block * SUBLANES
-            if block in PRODUCT_BLOCKS:
-                value = look_up_by_product(turned_ref, rank_ref, index_ref, first, cols)
-            else:
-                value = look_up(table_ref, index_ref[first : first + SUBLANES, cols])
-            permuted_ref[first : first + SUBLANES, cols] = value
-            for c in range(block * columns // blocks, (block + 1) * columns // blocks):
-                total = square[c]
+    order_rows(devices, block_rows, index_ref, ordered_ref)
+
+    def chunk_pair(i, carry):
+        for u in range(PAIR):
+            chunk_copy(i * PAIR + u).wait()
+        for u in look_up_pair(table_ref, turned_ref, rank_ref, ordered_ref, permuted_ref, half, i):
+            for c in range(columns):
+                total = square_ref[c * SUBLANES : (c + 1) * SUBLANES, :]
                 for r in range(0, LANES, 16):
-                    rows = pl.ds(pl.multiple_of(i * LANES + r, 16), 16)
+                    rows = pl.ds(pl.multiple_of((i * PAIR + u) * LANES + r, 16), 16)
                     wide = genotypes_ref[rows, c * LANES : (c + 1) * LANES].astype(jnp.float32)
                     wide = wide * wide
                     total = total + (wide[:SUBLANES] + wide[SUBLANES:])
-                new.append(total)
-        return tuple(new)
-
-    zero = jnp.zeros((SUBLANES, LANES), jnp.float32)
-    square = lax.fori_loop(0, chunks, one_chunk, (zero,) * columns)
+                square_ref[c * SUBLANES : (c + 1) * SUBLANES, :] = total
+        return carry
+
+    lax.fori_loop(0, chunks // PAIR, chunk_pair, 0)
+    square_row = (half + 1) * columns
     for c in range(columns):
-        sent_ref[square_row + c : square_row + c + 1, :] = jnp.sum(square[c], axis=0, keepdims=True)
-
-    source = source_rows(devices, block_rows, (perms, perms), 0)
-    choice = (source == lax.broadcasted_iota(jnp.int32, (perms, perms), 1)).astype(jnp.bfloat16)
-    ordered = jnp.dot(choice, permuted_ref[...].astype(jnp.bfloat16), preferred_element_type=jnp.float32).astype(jnp.bfloat16)
+        sent_ref[square_row + c : square_row + c + 1, :] = jnp.sum(
+            square_ref[c * SUBLANES : (c + 1) * SUBLANES, :], axis=0, keepdims=True
+        )
     ones = jnp.ones((16, local_count), jnp.bfloat16)
-    left = jnp.concatenate([ordered, ones], axis=0)
-    width = 2 * LANES
-    for first in range(0, variants, width):
-        product = jnp.dot(left, genotypes_ref[:, first : first + width], preferred_element_type=jnp.float32)
-        for c in range(first // LANES, (first + width) // LANES):
-            part = product[:, c * LANES - first : (c + 1) * LANES - first]
-            for r in range(0, half, SUBLANES):
-                rows = pl.ds(r * columns + c, SUBLANES, stride=columns)
-                kept_ref[rows, :] = part[r : r + SUBLANES]
-                sent_ref[rows, :] = part[half + r : half + r + SUBLANES]
-            sent_ref[count_row + c : count_row + c + 1, :] = part[perms : perms + 1]
+    multiply(jnp.concatenate([permuted_ref[...].astype(jnp.bfloat16), ones], axis=0), half, genotypes_ref, sent_ref)
+
+
+def rows_kernel(first_row, genotypes_ref, ordered_ref, table_ref, turned_ref, out_ref, rank_ref, permuted_ref):
+    chunks = permuted_ref.shape[1] // LANES
+    fill_ranks(rank_ref)
+
+    def chunk_pair(i, carry):
+        for _ in look_up_pair(table_ref, turned_ref, rank_ref, ordered_ref, permuted_ref, first_row, i):
+            pass
+        return carry
+
+    lax.fori_loop(0, chunks // PAIR, chunk_pair, 0)
+    multiply(permuted_ref[...].astype(jnp.bfloat16), permuted_ref.shape[0], genotypes_ref, out_ref)
 
 
 def final_kernel(samples, sigma2_ref, held_ref, moments_ref, *refs):
@@ -235,7 +260,7 @@
     count = sum((got_ref[kept : kept + columns, :] for got_ref in got_refs), moments_ref[:columns, :])
     square = sum((got_ref[kept + columns :, :] for got_ref in got_refs), moments_ref[columns:, :])
     spread = square - count * count / samples + 1.0
-    scale = jnp.sqrt(sigma2_ref[0] * spread)
+    scale = jnp.sqrt(sigma2_ref[:1, :] * spread)
     for r in range(block_rows):
         rows = slice(r * columns, (r + 1) * columns)
         statistic = sum((got_ref[rows, :] for got_ref in got_refs), held_ref[rows, :]) / scale
@@ -258,33 +283,57 @@
         pltpu.with_memory_space_constraint(array, pltpu.HBM)
         for array in (phenotype.reshape(table_rows, LANES), perm_index, genotypes)
     ]
-    kept = perms // 2 * columns
-    held, sent, sigma2 = pl.pallas_call(
-        functools.partial(partial_kernel, devices, block_rows),
+    half = perms // 2
+    kept = half * columns
+    widths = round_widths(devices)
+    sent, *shared, sigma2 = pl.pallas_call(
+        functools.partial(head_kernel, devices, block_rows),
         out_shape=(
-            jax.ShapeDtypeStruct((kept, LANES), jnp.float32),
             jax.ShapeDtypeStruct((kept + 2 * columns, LANES), jnp.float32),
-            jax.ShapeDtypeStruct((1,), jnp.float32),
+            jax.ShapeDtypeStruct(genotypes.shape, jnp.bfloat16),
+            jax.ShapeDtypeStruct(perm_index.shape, jnp.int32),
+            jax.ShapeDtypeStruct((table_rows // 2, LANES), jnp.int32),
+            jax.ShapeDtypeStruct((LANES, table_rows), jnp.bfloat16),
+            jax.ShapeDtypeStruct((SUBLANES, LANES), jnp.float32),
         ),
         in_specs=[pl.BlockSpec(memory_space=pltpu.HBM)] * 3,
-        out_specs=(vmem, vmem, smem),
+        out_specs=(vmem,) * 6,
         scratch_shapes=[
             pltpu.VMEM((table_rows, LANES), jnp.float32),
             pltpu.VMEM(perm_index.shape, jnp.int32),
-            pltpu.VMEM(genotypes.shape, jnp.bfloat16),
-            pltpu.VMEM((table_rows // 2, LANES), jnp.int32),
-            pltpu.VMEM((LANES, table_rows), jnp.bfloat16),
             pltpu.VMEM((table_rows, LANES), RANK),
-            pltpu.VMEM(perm_index.shape, jnp.float32),
+            pltpu.VMEM((half, local_count), jnp.float32),
+            pltpu.VMEM((columns * SUBLANES, LANES), jnp.float32),
             pltpu.SemaphoreType.DMA((local_count // LANES + 2,)),
         ],
         compiler_params=pltpu.CompilerParams(vmem_limit_bytes=16 << 20),
     )(*inputs)
 
+    def own_rows(first_row, rows):
+        return pl.pallas_call(
+            functools.partial(rows_kernel, first_row),
+            out_shape=jax.ShapeDtypeStruct((rows * columns, LANES), jnp.float32),
+            in_specs=[vmem] * 4,
+            out_specs=vmem,
+            scratch_shapes=[
+                pltpu.VMEM((table_rows, LANES), RANK),
+                pltpu.VMEM((rows, local_count), jnp.float32),
+            ],
+            compiler_params=pltpu.CompilerParams(vmem_limit_bytes=8 << 20),
+            cost_estimate=pl.CostEstimate(
+                flops=2 * rows * local_count * (samples + variants),
+                bytes_accessed=genotypes.size * 2,
+                transcendentals=0,
+            ),
+        )(*shared)
+
+    last = half >> widths[1]
+    onward = own_rows(last, half - last)
+    staying = own_rows(0, last)
+
     even, odd = (round_bits(devices, side) for side in (False, True))
     moments = sent[kept:]
     messages = [sent]
-    widths = round_widths(devices)
     done = 0
     for step, width in enumerate(widths):
         got = []
@@ -296,14 +345,19 @@
             got.append(lax.ppermute(message, "samp", pairs))
         done += width
         if done < len(even):
-            scores = sum((g[:kept] for g in got), held)
             moments = sum((g[kept:] for g in got), moments)
             following = widths[step + 1]
-            kept >>= following
-            held = scores[:kept]
+            first = kept >> following
+            if step == 0:
+                held = staying + got[0][:first]
+                scores = onward + got[0][first:kept]
+            else:
+                scores = sum((g[:kept] for g in got), held)
+                held, scores = scores[:first], scores[first:]
+            kept = first
             messages = [
                 jnp.concatenate([scores[part * kept : (part + 1) * kept], moments], axis=0)
-                for part in range(1, 1 << following)
+                for part in range((1 << following) - 1)
             ]
 
     statistic, largest = pl.pallas_call(
@@ -312,7 +366,7 @@
             jax.ShapeDtypeStruct((block_rows, variants), jnp.float32),
             jax.ShapeDtypeStruct((block_rows,), jnp.float32),
         ),
-        in_specs=[smem] + [vmem] * (2 + len(got)),
+        in_specs=[vmem] * (3 + len(got)),
         out_specs=(vmem, smem),
         compiler_params=pltpu.CompilerParams(vmem_limit_bytes=2 << 20),
     )(sigma2, held, moments, *got)

time: 32.2 us -> 30.2 us (0.938)
  waiting for transfers between devices: 10.5 us -> 7.2 us
  Pallas kernels: 11.2 us -> 13 us
  starting transfers between devices: 9.5 us -> 9.13 us
    ppermute x7, waiting for transfers between devices: 10.5 us -> 7.2 us  [on_device(): got.append(lax.ppermute(message, 'samp', pairs))]
    pallas_call x1 -> x3, Pallas kernels: 9.93 us -> 12.3 us  [the longest x1 6.6 us: on_device(): pl.pallas_call(functools.partial(head_kernel, devices, block_rows), out_s...]
    pallas_call x1, Pallas kernels: 1.28 us -> 0.66 us  [on_device(): pl.pallas_call(functools.partial(final_kernel, samples), out_shape=(jax.S...]
    ppermute x7, starting transfers between devices: 9.5 us -> 9.13 us  [on_device(): got.append(lax.ppermute(message, 'samp', pairs))]
  transfers between devices with their start and end apart: 7 -> 7, of which waited for: 7 -> 5; matrix products, arithmetic and copies ran while one was open for 0% -> 0% of each run, Pallas kernels for 0% -> 19%
where the time goes in v5:
time: 30.2 us; the launch traced here: 30.1 us
  Pallas kernels  13 us (43%)
  starting transfers between devices  9.13 us (30%)
  waiting for transfers between devices  7.2 us (24%)
  between operations  0.71 us (2%)
    ppermute x7, starting transfers between devices, on_device(): got.append(lax.ppermute(message, 'samp', pairs))  9.13 us
    ppermute x7, waiting for transfers between devices, on_device(): got.append(lax.ppermute(message, 'samp', pairs))  7.2 us
    pallas_call x1, Pallas kernels, on_device(): pl.pallas_call(functools.partial(head_kernel, devices, block_rows), out_s...  6.6 us
    pallas_call x2, Pallas kernels, own_rows(): pl.pallas_call(functools.partial(rows_kernel, first_row), out_shape=jax.S...  5.69 us
    pallas_call x1, Pallas kernels, on_device(): pl.pallas_call(functools.partial(final_kernel, samples), out_shape=(jax.S...  0.66 us
  transfers between devices with their start and end apart: 7, of which 5 were waited for; matrix products, arithmetic and copies ran while one was open for 0% of the time, Pallas kernels for 19%

profile of v5, /device:TPU:0, one launch (start us, length us, event | category | flops | bytes accessed | tf_op | source)
XLA Modules:
  0.0 30.1 jit_solution(16393306854966224177)
XLA Ops:
  0.6 6.6 %shard_map.50 = (f32[544,128]{1,0:T(8,128)S(1)}, bf16[1024,2048]{1,0:T(8,128)(2,1)S(1)}, s32[64,1024]{1,0:T(8,128)S(1)}, s32[128,128]{1,0:T(8,128)S(1)}, bf16[12...) custom-call(f32[256,128]{1,0:T(8,128)} %bitcast.1, s32[64,1024]{1,0:T(8,128)} %index_hbm.1, bf16[1024,2048]{1,0:T(8,128)(2,1)} %genotypes_hbm.1), custom_call_target="tpu_custom_call" | custom-call | tf_op jit(solution)/shard_map/pallas_call | solution.py:289
  7.2 0.6 %collective-permute-start = (f32[544,128]{1,0:T(8,128)S(1)}, f32[544,128]{1,0:T(8,128)S(1)}, u32[]{:S(2)}, u32[]{:S(2)}) collective-permute-start(f32[544,128]{1,0:T(8,128)S(1)} %get-tuple-element.13), channel_id=1, source_target_pairs={{0,1},{1,0},{2,3},{3,2},{4,5},{5,4},{6,7},{7,6},{8,9},{9,8},{10,11... | collective-permute-start | bytes 835592 | tf_op jit(solution)/shard_map/ppermute | solution.py:345
  7.8 3.6 %shard_map.52 = f32[384,128]{1,0:T(8,128)S(1)} custom-call(bf16[1024,2048]{1,0:T(8,128)(2,1)S(1)} %get-tuple-element.9.genotypes_ref, s32[64,1024]{1,0:T(8,128)S(1)} %get-tuple-element.10.ordered_ref, s32[128,128]{1,0:T(8,128)S(1)} %get-tuple-element.11.table_ref, bf16[128,256]{1,0:T(8,128)(2,1)S(1)} %get-tuple-element.12.turned_ref), custom_call_target="tpu_custom_call" | custom-call | flops 1711276032 | bytes 4194304 | tf_op jit(solution)/shard_map/pallas_call | solution.py:313
  11.4 0.0 collective-permute-done
  11.5 2.6 %collective-permute-start.1 = (f32[160,128]{1,0:T(8,128)S(1)}, f32[160,128]{1,0:T(8,128)S(1)}, u32[]{:S(2)}, u32[]{:S(2)}) collective-permute-start(f32[160,128]{1,0:T(8,128)S(1)} %get-tuple-element.24), channel_id=1, source_target_pairs={{0,4},{1,3},{2,6},{3,1},{4,0},{5,7},{6,2},{7,5},{8,12},{9,11},{10,... | collective-permute-start | bytes 245768 | tf_op jit(solution)/shard_map/ppermute | solution.py:345
  14.1 1.5 %collective-permute-start.2 = (f32[160,128]{1,0:T(8,128)S(1)}, f32[160,128]{1,0:T(8,128)S(1)}, u32[]{:S(2)}, u32[]{:S(2)}) collective-permute-start(f32[160,128]{1,0:T(8,128)S(1)} %get-tuple-element.25), channel_id=1, source_target_pairs={{0,2},{1,5},{2,0},{3,7},{4,6},{5,1},{6,4},{7,3},{8,10},{9,13},{10,... | collective-permute-start | bytes 245768 | tf_op jit(solution)/shard_map/ppermute | solution.py:345
  15.6 0.0 collective-permute-start.3
  15.6 2.1 %shard_map.51 = f32[128,128]{1,0:T(8,128)S(1)} custom-call(bf16[1024,2048]{1,0:T(8,128)(2,1)S(1)} %get-tuple-element.9.genotypes_ref, s32[64,1024]{1,0:T(8,128)S(1)} %get-tuple-element.10.ordered_ref, s32[128,128]{1,0:T(8,128)S(1)} %get-tuple-element.11.table_ref, bf16[128,256]{1,0:T(8,128)(2,1)S(1)} %get-tuple-element.12.turned_ref), custom_call_target="tpu_custom_call" | custom-call | flops 570425344 | bytes 4194304 | tf_op jit(solution)/shard_map/pallas_call | solution.py:313
  17.7 0.0 collective-permute-done.1
  17.7 1.2 %collective-permute-done.2 = f32[160,128]{1,0:T(8,128)S(1)} collective-permute-done((f32[160,128]{1,0:T(8,128)S(1)}, f32[160,128]{1,0:T(8,128)S(1)}, u32[]{:S(2)}, u32[]{:S(2)}) %collective-permute-start.2) | collective-permute-done | bytes 81952 | tf_op jit(solution)/shard_map/ppermute | solution.py:345
  19.0 1.9 %collective-permute-done.3 = f32[160,128]{1,0:T(8,128)S(1)} collective-permute-done((f32[160,128]{1,0:T(8,128)S(1)}, f32[160,128]{1,0:T(8,128)S(1)}, u32[]{:S(2)}, u32[]{:S(2)}) %collective-permute-start.3) | collective-permute-done | bytes 81952 | tf_op jit(solution)/shard_map/ppermute | solution.py:345
  21.0 3.7 %collective-permute-start.6 = (f32[64,128]{1,0:T(8,128)S(1)}, f32[64,128]{1,0:T(8,128)S(1)}, u32[]{:S(2)}, u32[]{:S(2)}) collective-permute-start(f32[64,128]{1,0:T(8,128)S(1)} %get-tuple-element.21), channel_id=1, source_target_pairs={{0,24},{1,25},{2,26},{3,27},{4,28},{5,29},{6,30},{7,31},{8,16},{9,... | collective-permute-start | bytes 98312 | tf_op jit(solution)/shard_map/ppermute | solution.py:345
  24.6 0.0 collective-permute-start.5
  24.6 0.8 %collective-permute-start.4 = (f32[64,128]{1,0:T(8,128)S(1)}, f32[64,128]{1,0:T(8,128)S(1)}, u32[]{:S(2)}, u32[]{:S(2)}) collective-permute-start(f32[64,128]{1,0:T(8,128)S(1)} %get-tuple-element.23), channel_id=1, source_target_pairs={{0,16},{1,17},{2,18},{3,19},{4,20},{5,21},{6,22},{7,23},{8,24},{9,... | collective-permute-start | bytes 98312 | tf_op jit(solution)/shard_map/ppermute | solution.py:345
  25.4 1.3 %collective-permute-done.6.refs_2_ = f32[64,128]{1,0:T(8,128)S(1)} collective-permute-done((f32[64,128]{1,0:T(8,128)S(1)}, f32[64,128]{1,0:T(8,128)S(1)}, u32[]{:S(2)}, u32[]{:S(2)}) %collective-permute-start.6) | collective-permute-done | bytes 32800 | tf_op jit(solution)/shard_map/ppermute | solution.py:345
  26.7 1.8 %collective-permute-done.5.refs_1_ = f32[64,128]{1,0:T(8,128)S(1)} collective-permute-done((f32[64,128]{1,0:T(8,128)S(1)}, f32[64,128]{1,0:T(8,128)S(1)}, u32[]{:S(2)}, u32[]{:S(2)}) %collective-permute-start.5) | collective-permute-done | bytes 32800 | tf_op jit(solution)/shard_map/ppermute | solution.py:345
  28.5 0.9 %collective-permute-done.4.refs_0_ = f32[64,128]{1,0:T(8,128)S(1)} collective-permute-done((f32[64,128]{1,0:T(8,128)S(1)}, f32[64,128]{1,0:T(8,128)S(1)}, u32[]{:S(2)}, u32[]{:S(2)}) %collective-permute-start.4) | collective-permute-done | bytes 32800 | tf_op jit(solution)/shard_map/ppermute | solution.py:345
  29.4 0.7 %shard_map.53 = (f32[2,2048]{1,0:T(2,128)}, f32[2]{0:T(128)}) custom-call(f32[8,128]{1,0:T(8,128)S(1)} %get-tuple-element.8.sigma2_ref, f32[32,128]{1,0:T(8,128)S(1)} %get-tuple-element.20.held_ref, f32[32,128]{1,0:T(8,128)S(1)} %get-tuple-element.27.moments_ref, f32[64,128]{1,0:T(8,128)S(1)} %collective-permute-done.4.refs_0_, ...), custom_call_target="tpu_custom_call" | custom-call | tf_op jit(solution)/shard_map/pallas_call | solution.py:363
  (7 shorter events, 0.1 us)
Async XLA Ops:
  7.2 4.1 %collective-permute-start = (f32[544,128]{1,0:T(8,128)S(1)}, f32[544,128]{1,0:T(8,128)S(1)}, u32[]{:S(2)}, u32[]{:S(2)}) collective-permute-start(f32[544,128]{1,0:T(8,128)S(1)} %get-tuple-element.13), channel_id=1, source_target_pairs={{0,1},{1,0},{2,3},{3,2},{4,5},{5,4},{6,7},{7,6},{8,9},{9,8},{10,11... | collective-permute-start | bytes 835592 | tf_op jit(solution)/shard_map/ppermute | solution.py:345
  11.5 6.2 %collective-permute-start.1 = (f32[160,128]{1,0:T(8,128)S(1)}, f32[160,128]{1,0:T(8,128)S(1)}, u32[]{:S(2)}, u32[]{:S(2)}) collective-permute-start(f32[160,128]{1,0:T(8,128)S(1)} %get-tuple-element.24), channel_id=1, source_target_pairs={{0,4},{1,3},{2,6},{3,1},{4,0},{5,7},{6,2},{7,5},{8,12},{9,11},{10,... | collective-permute-start | bytes 245768 | tf_op jit(solution)/shard_map/ppermute | solution.py:345
  14.1 4.9 %collective-permute-start.2 = (f32[160,128]{1,0:T(8,128)S(1)}, f32[160,128]{1,0:T(8,128)S(1)}, u32[]{:S(2)}, u32[]{:S(2)}) collective-permute-start(f32[160,128]{1,0:T(8,128)S(1)} %get-tuple-element.25), channel_id=1, source_target_pairs={{0,2},{1,5},{2,0},{3,7},{4,6},{5,1},{6,4},{7,3},{8,10},{9,13},{10,... | collective-permute-start | bytes 245768 | tf_op jit(solution)/shard_map/ppermute | solution.py:345
  15.6 5.3 %collective-permute-start.3 = (f32[160,128]{1,0:T(8,128)S(1)}, f32[160,128]{1,0:T(8,128)S(1)}, u32[]{:S(2)}, u32[]{:S(2)}) collective-permute-start(f32[160,128]{1,0:T(8,128)S(1)} %get-tuple-element.26), channel_id=1, source_target_pairs={{0,6},{1,7},{2,4},{3,5},{4,2},{5,3},{6,0},{7,1},{8,14},{9,15},{10,... | collective-permute-start | bytes 245768 | tf_op jit(solution)/shard_map/ppermute | solution.py:345
  21.0 5.8 %collective-permute-start.6 = (f32[64,128]{1,0:T(8,128)S(1)}, f32[64,128]{1,0:T(8,128)S(1)}, u32[]{:S(2)}, u32[]{:S(2)}) collective-permute-start(f32[64,128]{1,0:T(8,128)S(1)} %get-tuple-element.21), channel_id=1, source_target_pairs={{0,24},{1,25},{2,26},{3,27},{4,28},{5,29},{6,30},{7,31},{8,16},{9,... | collective-permute-start | bytes 98312 | tf_op jit(solution)/shard_map/ppermute | solution.py:345
  24.6 3.9 %collective-permute-start.5 = (f32[64,128]{1,0:T(8,128)S(1)}, f32[64,128]{1,0:T(8,128)S(1)}, u32[]{:S(2)}, u32[]{:S(2)}) collective-permute-start(f32[64,128]{1,0:T(8,128)S(1)} %get-tuple-element.22), channel_id=1, source_target_pairs={{0,8},{1,9},{2,10},{3,11},{4,12},{5,13},{6,14},{7,15},{8,0},{9,1},... | collective-permute-start | bytes 98312 | tf_op jit(solution)/shard_map/ppermute | solution.py:345
  24.6 4.8 %collective-permute-start.4 = (f32[64,128]{1,0:T(8,128)S(1)}, f32[64,128]{1,0:T(8,128)S(1)}, u32[]{:S(2)}, u32[]{:S(2)}) collective-permute-start(f32[64,128]{1,0:T(8,128)S(1)} %get-tuple-element.23), channel_id=1, source_target_pairs={{0,16},{1,17},{2,18},{3,19},{4,20},{5,21},{6,22},{7,23},{8,24},{9,... | collective-permute-start | bytes 98312 | tf_op jit(solution)/shard_map/ppermute | solution.py:345

commit v6 on v5

--- a/solution.py
+++ b/solution.py
@@ -6,6 +6,7 @@
 from jax.experimental import pallas as pl
 from jax.experimental.pallas import tpu as pltpu
 from jax.sharding import PartitionSpec as P
+
 
 LANES = 128
 SUBLANES = 8
@@ -155,7 +156,7 @@
             else:
                 value = look_up(table_ref, index_ref[first : first + SUBLANES, cols])
             permuted_ref[block * SUBLANES : (block + 1) * SUBLANES, cols] = value
-        yield u
+            yield u, block, value
 
 
 def multiply(left, rows, genotypes_ref, out_ref):
@@ -181,7 +182,7 @@
     table_rows = phenotype_ref.shape[0]
     samples = table_rows * LANES
     words = table_ref.shape[0]
-    half = perms // 2
+    rows_sent = permuted_ref.shape[0]
 
     def chunk_copy(i):
         rows = pl.ds(pl.multiple_of(i * LANES, LANES), LANES)
@@ -218,25 +219,30 @@
     def chunk_pair(i, carry):
         for u in range(PAIR):
             chunk_copy(i * PAIR + u).wait()
-        for u in look_up_pair(table_ref, turned_ref, rank_ref, ordered_ref, permuted_ref, half, i):
-            for c in range(columns):
-                total = square_ref[c * SUBLANES : (c + 1) * SUBLANES, :]
+        blocks = rows_sent // SUBLANES
+        after = jnp.zeros((SUBLANES, LANES), jnp.float32)
+        for u, block, value in look_up_pair(
+            table_ref, turned_ref, rank_ref, ordered_ref, permuted_ref, perms - rows_sent, i
+        ):
+            for c in range(block * columns // blocks, (block + 1) * columns // blocks):
+                total = square_ref[c * SUBLANES : (c + 1) * SUBLANES, :] + after
                 for r in range(0, LANES, 16):
                     rows = pl.ds(pl.multiple_of((i * PAIR + u) * LANES + r, 16), 16)
                     wide = genotypes_ref[rows, c * LANES : (c + 1) * LANES].astype(jnp.float32)
                     wide = wide * wide
                     total = total + (wide[:SUBLANES] + wide[SUBLANES:])
                 square_ref[c * SUBLANES : (c + 1) * SUBLANES, :] = total
+            after = value * 0.0
         return carry
 
     lax.fori_loop(0, chunks // PAIR, chunk_pair, 0)
-    square_row = (half + 1) * columns
+    square_row = (rows_sent + 1) * columns
     for c in range(columns):
         sent_ref[square_row + c : square_row + c + 1, :] = jnp.sum(
             square_ref[c * SUBLANES : (c + 1) * SUBLANES, :], axis=0, keepdims=True
         )
     ones = jnp.ones((16, local_count), jnp.bfloat16)
-    multiply(jnp.concatenate([permuted_ref[...].astype(jnp.bfloat16), ones], axis=0), half, genotypes_ref, sent_ref)
+    multiply(jnp.concatenate([permuted_ref[...].astype(jnp.bfloat16), ones], axis=0), rows_sent, genotypes_ref, sent_ref)
 
 
 def rows_kernel(first_row, genotypes_ref, ordered_ref, table_ref, turned_ref, out_ref, rank_ref, permuted_ref):
@@ -284,8 +290,9 @@
         for array in (phenotype.reshape(table_rows, LANES), perm_index, genotypes)
     ]
     half = perms // 2
-    kept = half * columns
     widths = round_widths(devices)
+    last = half >> widths[1]
+    kept = (half - last) * columns
     sent, *shared, sigma2 = pl.pallas_call(
         functools.partial(head_kernel, devices, block_rows),
         out_shape=(
@@ -302,7 +309,7 @@
             pltpu.VMEM((table_rows, LANES), jnp.float32),
             pltpu.VMEM(perm_index.shape, jnp.int32),
             pltpu.VMEM((table_rows, LANES), RANK),
-            pltpu.VMEM((half, local_count), jnp.float32),
+            pltpu.VMEM((half - last, local_count), jnp.float32),
             pltpu.VMEM((columns * SUBLANES, LANES), jnp.float32),
             pltpu.SemaphoreType.DMA((local_count // LANES + 2,)),
         ],
@@ -327,9 +334,9 @@
             ),
         )(*shared)
 
-    last = half >> widths[1]
     onward = own_rows(last, half - last)
     staying = own_rows(0, last)
+    crossing = own_rows(half, last)
 
     even, odd = (round_bits(devices, side) for side in (False, True))
     moments = sent[kept:]
@@ -349,8 +356,9 @@
             following = widths[step + 1]
             first = kept >> following
             if step == 0:
-                held = staying + got[0][:first]
-                scores = onward + got[0][first:kept]
+                first = last * columns
+                held = staying + lax.ppermute(crossing, "samp", pairs)
+                scores = onward + got[0][:kept]
             else:
                 scores = sum((g[:kept] for g in got), held)
                 held, scores = scores[:first], scores[first:]
@@ -377,6 +385,7 @@
 
 def solution(mesh):
     placed = (P(), P(None, "samp"), P("samp", "var"))
+
     return jax.shard_map(
         on_device,
         mesh=mesh,

time: 30.2 us -> 29.8 us (0.987)
  waiting for transfers between devices: 7.2 us -> 5.89 us
  Pallas kernels: 13 us -> 13.7 us
    pallas_call x2 -> x3, Pallas kernels: 5.69 us -> 7.83 us  [own_rows(): pl.pallas_call(functools.partial(rows_kernel, first_row), out_shape=jax.S...]
    pallas_call x1, Pallas kernels: 6.6 us -> 5.22 us  [on_device(): pl.pallas_call(functools.partial(head_kernel, devices, block_rows), out_s...]
    ppermute x7, waiting for transfers between devices: 7.2 us -> 5.89 us  [on_device(): got.append(lax.ppermute(message, 'samp', pairs))]
  transfers between devices with their start and end apart: 7 -> 8, of which waited for: 5 -> 4; matrix products, arithmetic and copies ran while one was open for 0% -> 0% of each run, Pallas kernels for 19% -> 26%
where the time goes in v6:
time: 29.8 us; the launch traced here: 29.6 us
  Pallas kernels  13.7 us (46%)
  starting transfers between devices  9.2 us (31%)
  waiting for transfers between devices  5.89 us (20%)
  between operations  0.73 us (2%)
    ppermute x7, starting transfers between devices, on_device(): got.append(lax.ppermute(message, 'samp', pairs))  9.2 us
    pallas_call x3, Pallas kernels, own_rows(): pl.pallas_call(functools.partial(rows_kernel, first_row), out_shape=jax.S...  7.83 us
    ppermute x7, waiting for transfers between devices, on_device(): got.append(lax.ppermute(message, 'samp', pairs))  5.89 us
    pallas_call x1, Pallas kernels, on_device(): pl.pallas_call(functools.partial(head_kernel, devices, block_rows), out_s...  5.22 us
    pallas_call x1, Pallas kernels, on_device(): pl.pallas_call(functools.partial(final_kernel, samples), out_shape=(jax.S...  0.66 us
  transfers between devices with their start and end apart: 8, of which 4 were waited for; matrix products, arithmetic and copies ran while one was open for 0% of the time, Pallas kernels for 26%

profile of v6, /device:TPU:0, one launch (start us, length us, event | category | flops | bytes accessed | tf_op | source)
XLA Modules:
  0.0 29.6 jit_solution(2555614781368722129)
XLA Ops:
  0.6 5.2 %shard_map.50 = (f32[416,128]{1,0:T(8,128)S(1)}, bf16[1024,2048]{1,0:T(8,128)(2,1)S(1)}, s32[64,1024]{1,0:T(8,128)S(1)}, s32[128,128]{1,0:T(8,128)S(1)}, bf16[12...) custom-call(f32[256,128]{1,0:T(8,128)} %bitcast.1, s32[64,1024]{1,0:T(8,128)} %index_hbm.1, bf16[1024,2048]{1,0:T(8,128)(2,1)} %genotypes_hbm.1), custom_call_target="tpu_custom_call" | custom-call | tf_op jit(solution)/shard_map/pallas_call | solution.py:296
  5.9 0.6 %collective-permute-start.1 = (f32[416,128]{1,0:T(8,128)S(1)}, f32[416,128]{1,0:T(8,128)S(1)}, u32[]{:S(2)}, u32[]{:S(2)}) collective-permute-start(f32[416,128]{1,0:T(8,128)S(1)} %get-tuple-element.13), channel_id=1, source_target_pairs={{0,1},{1,0},{2,3},{3,2},{4,5},{5,4},{6,7},{7,6},{8,9},{9,8},{10,11... | collective-permute-start | bytes 638984 | tf_op jit(solution)/shard_map/ppermute | solution.py:352
  6.4 3.6 %shard_map.53 = f32[384,128]{1,0:T(8,128)S(1)} custom-call(bf16[1024,2048]{1,0:T(8,128)(2,1)S(1)} %get-tuple-element.9.genotypes_ref, s32[64,1024]{1,0:T(8,128)S(1)} %get-tuple-element.10.ordered_ref, s32[128,128]{1,0:T(8,128)S(1)} %get-tuple-element.11.table_ref, bf16[128,256]{1,0:T(8,128)(2,1)S(1)} %get-tuple-element.12.turned_ref), custom_call_target="tpu_custom_call" | custom-call | flops 1711276032 | bytes 4194304 | tf_op jit(solution)/shard_map/pallas_call | solution.py:320
  10.0 0.0 collective-permute-done.1
  10.1 3.5 %collective-permute-start.4 = (f32[160,128]{1,0:T(8,128)S(1)}, f32[160,128]{1,0:T(8,128)S(1)}, u32[]{:S(2)}, u32[]{:S(2)}) collective-permute-start(f32[160,128]{1,0:T(8,128)S(1)} %get-tuple-element.26), channel_id=1, source_target_pairs={{0,6},{1,7},{2,4},{3,5},{4,2},{5,3},{6,0},{7,1},{8,14},{9,15},{10,... | collective-permute-start | bytes 245768 | tf_op jit(solution)/shard_map/ppermute | solution.py:352
  13.6 0.5 %collective-permute-start.3 = (f32[160,128]{1,0:T(8,128)S(1)}, f32[160,128]{1,0:T(8,128)S(1)}, u32[]{:S(2)}, u32[]{:S(2)}) collective-permute-start(f32[160,128]{1,0:T(8,128)S(1)} %get-tuple-element.25), channel_id=1, source_target_pairs={{0,2},{1,5},{2,0},{3,7},{4,6},{5,1},{6,4},{7,3},{8,10},{9,13},{10,... | collective-permute-start | bytes 245768 | tf_op jit(solution)/shard_map/ppermute | solution.py:352
  14.1 0.1 collective-permute-start.2
  14.3 2.1 %shard_map.52 = f32[128,128]{1,0:T(8,128)S(1)} custom-call(bf16[1024,2048]{1,0:T(8,128)(2,1)S(1)} %get-tuple-element.9.genotypes_ref, s32[64,1024]{1,0:T(8,128)S(1)} %get-tuple-element.10.ordered_ref, s32[128,128]{1,0:T(8,128)S(1)} %get-tuple-element.11.table_ref, bf16[128,256]{1,0:T(8,128)(2,1)S(1)} %get-tuple-element.12.turned_ref), custom_call_target="tpu_custom_call" | custom-call | flops 570425344 | bytes 4194304 | tf_op jit(solution)/shard_map/pallas_call | solution.py:320
  16.4 0.0 collective-permute-start
  16.4 2.1 %shard_map.51 = f32[128,128]{1,0:T(8,128)S(1)} custom-call(bf16[1024,2048]{1,0:T(8,128)(2,1)S(1)} %get-tuple-element.9.genotypes_ref, s32[64,1024]{1,0:T(8,128)S(1)} %get-tuple-element.10.ordered_ref, s32[128,128]{1,0:T(8,128)S(1)} %get-tuple-element.11.table_ref, bf16[128,256]{1,0:T(8,128)(2,1)S(1)} %get-tuple-element.12.turned_ref), custom_call_target="tpu_custom_call" | custom-call | flops 570425344 | bytes 4194304 | tf_op jit(solution)/shard_map/pallas_call | solution.py:320
  18.5 0.0 collective-permute-done
  18.5 0.0 collective-permute-done.4
  18.5 0.2 collective-permute-done.3
  18.7 0.0 collective-permute-done.2
  18.8 2.9 %collective-permute-start.5 = (f32[64,128]{1,0:T(8,128)S(1)}, f32[64,128]{1,0:T(8,128)S(1)}, u32[]{:S(2)}, u32[]{:S(2)}) collective-permute-start(f32[64,128]{1,0:T(8,128)S(1)} %get-tuple-element.23), channel_id=1, source_target_pairs={{0,16},{1,17},{2,18},{3,19},{4,20},{5,21},{6,22},{7,23},{8,24},{9,... | collective-permute-start | bytes 98312 | tf_op jit(solution)/shard_map/ppermute | solution.py:352
  21.7 1.6 %collective-permute-start.6 = (f32[64,128]{1,0:T(8,128)S(1)}, f32[64,128]{1,0:T(8,128)S(1)}, u32[]{:S(2)}, u32[]{:S(2)}) collective-permute-start(f32[64,128]{1,0:T(8,128)S(1)} %get-tuple-element.22), channel_id=1, source_target_pairs={{0,8},{1,9},{2,10},{3,11},{4,12},{5,13},{6,14},{7,15},{8,0},{9,1},... | collective-permute-start | bytes 98312 | tf_op jit(solution)/shard_map/ppermute | solution.py:352
  23.3 0.0 collective-permute-start.7
  23.3 0.5 %collective-permute-done.5.refs_0_ = f32[64,128]{1,0:T(8,128)S(1)} collective-permute-done((f32[64,128]{1,0:T(8,128)S(1)}, f32[64,128]{1,0:T(8,128)S(1)}, u32[]{:S(2)}, u32[]{:S(2)}) %collective-permute-start.5) | collective-permute-done | bytes 32800 | tf_op jit(solution)/shard_map/ppermute | solution.py:352
  23.8 1.9 %collective-permute-done.6.refs_1_ = f32[64,128]{1,0:T(8,128)S(1)} collective-permute-done((f32[64,128]{1,0:T(8,128)S(1)}, f32[64,128]{1,0:T(8,128)S(1)}, u32[]{:S(2)}, u32[]{:S(2)}) %collective-permute-start.6) | collective-permute-done | bytes 32800 | tf_op jit(solution)/shard_map/ppermute | solution.py:352
  25.6 3.4 %collective-permute-done.7.refs_2_ = f32[64,128]{1,0:T(8,128)S(1)} collective-permute-done((f32[64,128]{1,0:T(8,128)S(1)}, f32[64,128]{1,0:T(8,128)S(1)}, u32[]{:S(2)}, u32[]{:S(2)}) %collective-permute-start.7) | collective-permute-done | bytes 32800 | tf_op jit(solution)/shard_map/ppermute | solution.py:352
  29.0 0.7 %shard_map.54 = (f32[2,2048]{1,0:T(2,128)}, f32[2]{0:T(128)}) custom-call(f32[8,128]{1,0:T(8,128)S(1)} %get-tuple-element.8.sigma2_ref, f32[32,128]{1,0:T(8,128)S(1)} %get-tuple-element.20.held_ref, f32[32,128]{1,0:T(8,128)S(1)} %slice_add_fusion.4.moments_ref, f32[64,128]{1,0:T(8,128)S(1)} %collective-permute-done.5.refs_0_, ...), custom_call_target="tpu_custom_call" | custom-call | tf_op jit(solution)/shard_map/pallas_call | solution.py:371
  (8 shorter events, 0.1 us)
Async XLA Ops:
  5.9 4.1 %collective-permute-start.1 = (f32[416,128]{1,0:T(8,128)S(1)}, f32[416,128]{1,0:T(8,128)S(1)}, u32[]{:S(2)}, u32[]{:S(2)}) collective-permute-start(f32[416,128]{1,0:T(8,128)S(1)} %get-tuple-element.13), channel_id=1, source_target_pairs={{0,1},{1,0},{2,3},{3,2},{4,5},{5,4},{6,7},{7,6},{8,9},{9,8},{10,11... | collective-permute-start | bytes 638984 | tf_op jit(solution)/shard_map/ppermute | solution.py:352
  10.1 8.4 %collective-permute-start.4 = (f32[160,128]{1,0:T(8,128)S(1)}, f32[160,128]{1,0:T(8,128)S(1)}, u32[]{:S(2)}, u32[]{:S(2)}) collective-permute-start(f32[160,128]{1,0:T(8,128)S(1)} %get-tuple-element.26), channel_id=1, source_target_pairs={{0,6},{1,7},{2,4},{3,5},{4,2},{5,3},{6,0},{7,1},{8,14},{9,15},{10,... | collective-permute-start | bytes 245768 | tf_op jit(solution)/shard_map/ppermute | solution.py:352
  13.6 5.1 %collective-permute-start.3 = (f32[160,128]{1,0:T(8,128)S(1)}, f32[160,128]{1,0:T(8,128)S(1)}, u32[]{:S(2)}, u32[]{:S(2)}) collective-permute-start(f32[160,128]{1,0:T(8,128)S(1)} %get-tuple-element.25), channel_id=1, source_target_pairs={{0,2},{1,5},{2,0},{3,7},{4,6},{5,1},{6,4},{7,3},{8,10},{9,13},{10,... | collective-permute-start | bytes 245768 | tf_op jit(solution)/shard_map/ppermute | solution.py:352
  14.1 4.6 %collective-permute-start.2 = (f32[160,128]{1,0:T(8,128)S(1)}, f32[160,128]{1,0:T(8,128)S(1)}, u32[]{:S(2)}, u32[]{:S(2)}) collective-permute-start(f32[160,128]{1,0:T(8,128)S(1)} %get-tuple-element.24), channel_id=1, source_target_pairs={{0,4},{1,3},{2,6},{3,1},{4,0},{5,7},{6,2},{7,5},{8,12},{9,11},{10,... | collective-permute-start | bytes 245768 | tf_op jit(solution)/shard_map/ppermute | solution.py:352
  16.4 2.1 %collective-permute-start = (f32[128,128]{1,0:T(8,128)S(1)}, f32[128,128]{1,0:T(8,128)S(1)}, u32[]{:S(2)}, u32[]{:S(2)}) collective-permute-start(f32[128,128]{1,0:T(8,128)S(1)} %shard_map.52), channel_id=1, source_target_pairs={{0,1},{1,0},{2,3},{3,2},{4,5},{5,4},{6,7},{7,6},{8,9},{9,8},{10,11... | collective-permute-start | bytes 196616 | tf_op jit(solution)/shard_map/ppermute | solution.py:360
  18.8 5.0 %collective-permute-start.5 = (f32[64,128]{1,0:T(8,128)S(1)}, f32[64,128]{1,0:T(8,128)S(1)}, u32[]{:S(2)}, u32[]{:S(2)}) collective-permute-start(f32[64,128]{1,0:T(8,128)S(1)} %get-tuple-element.23), channel_id=1, source_target_pairs={{0,16},{1,17},{2,18},{3,19},{4,20},{5,21},{6,22},{7,23},{8,24},{9,... | collective-permute-start | bytes 98312 | tf_op jit(solution)/shard_map/ppermute | solution.py:352
  21.7 3.9 %collective-permute-start.6 = (f32[64,128]{1,0:T(8,128)S(1)}, f32[64,128]{1,0:T(8,128)S(1)}, u32[]{:S(2)}, u32[]{:S(2)}) collective-permute-start(f32[64,128]{1,0:T(8,128)S(1)} %get-tuple-element.22), channel_id=1, source_target_pairs={{0,8},{1,9},{2,10},{3,11},{4,12},{5,13},{6,14},{7,15},{8,0},{9,1},... | collective-permute-start | bytes 98312 | tf_op jit(solution)/shard_map/ppermute | solution.py:352
  23.3 5.7 %collective-permute-start.7 = (f32[64,128]{1,0:T(8,128)S(1)}, f32[64,128]{1,0:T(8,128)S(1)}, u32[]{:S(2)}, u32[]{:S(2)}) collective-permute-start(f32[64,128]{1,0:T(8,128)S(1)} %get-tuple-element.21), channel_id=1, source_target_pairs={{0,24},{1,25},{2,26},{3,27},{4,28},{5,29},{6,30},{7,31},{8,16},{9,... | collective-permute-start | bytes 98312 | tf_op jit(solution)/shard_map/ppermute | solution.py:352

commit v7 on v6

--- a/solution.py
+++ b/solution.py
@@ -11,7 +11,9 @@
 LANES = 128
 SUBLANES = 8
 RANK = jnp.bfloat16
-PAIR = 2
+PRODUCTS = 3
+SPLIT = 8
+FETCHED = (2,)
 WIDTHS = (1, 2, 2)
 
 LANE_GATHER = lax.GatherDimensionNumbers(
@@ -145,18 +147,17 @@
         rank_ref[r : r + 16, :] = rank.astype(jnp.float32).astype(RANK)
 
 
-def look_up_pair(table_ref, turned_ref, rank_ref, index_ref, permuted_ref, first_row, i):
+def look_up_chunk(table_ref, turned_ref, rank_ref, index_ref, permuted_ref, first_row, i):
     blocks = permuted_ref.shape[0] // SUBLANES
-    for u in range(PAIR):
-        cols = pl.ds(pl.multiple_of((i * PAIR + u) * LANES, LANES), LANES)
-        for block in range(blocks):
-            first = first_row + block * SUBLANES
-            if ((u * blocks + block) * 3) % 8 < 3:
-                value = look_up_by_product(turned_ref, rank_ref, index_ref, first, cols)
-            else:
-                value = look_up(table_ref, index_ref[first : first + SUBLANES, cols])
-            permuted_ref[block * SUBLANES : (block + 1) * SUBLANES, cols] = value
-            yield u, block, value
+    cols = slice(i * LANES, (i + 1) * LANES)
+    for block in range(blocks):
+        first = first_row + block * SUBLANES
+        if ((i * blocks + block) * PRODUCTS) % 8 < PRODUCTS:
+            value = look_up_by_product(turned_ref, rank_ref, index_ref, first, cols)
+        else:
+            value = look_up(table_ref, index_ref[first : first + SUBLANES, cols])
+        permuted_ref[block * SUBLANES : (block + 1) * SUBLANES, cols] = value
+        yield value
 
 
 def multiply(left, rows, genotypes_ref, out_ref):
@@ -216,26 +217,35 @@
     index_copy.wait()
     order_rows(devices, block_rows, index_ref, ordered_ref)
 
-    def chunk_pair(i, carry):
-        for u in range(PAIR):
-            chunk_copy(i * PAIR + u).wait()
-        blocks = rows_sent // SUBLANES
+    def add_squares(i, c, after):
+        total = square_ref[c * SUBLANES : (c + 1) * SUBLANES, :] + after
+        for r in range(i * LANES, (i + 1) * LANES, 16):
+            wide = genotypes_ref[r : r + 16, c * LANES : (c + 1) * LANES].astype(jnp.float32)
+            wide = wide * wide
+            total = total + (wide[:SUBLANES] + wide[SUBLANES:])
+        square_ref[c * SUBLANES : (c + 1) * SUBLANES, :] = total
+
+    blocks = rows_sent // SUBLANES
+    starts = [chunks * k // SPLIT for k in FETCHED] + [chunks]
+    arrived = [chunks * k // (len(FETCHED)) for k in range(len(FETCHED) + 1)]
+    for part in range(-1, len(FETCHED)):
+        first, end = (starts[part], starts[part + 1]) if part >= 0 else (0, starts[0])
+        work = []
+        if part >= 0:
+            for i in range(arrived[part], arrived[part + 1]):
+                chunk_copy(i).wait()
+                work += [(i, c) for c in range(columns)]
+        slots = (end - first) * blocks
+        done = 0
         after = jnp.zeros((SUBLANES, LANES), jnp.float32)
-        for u, block, value in look_up_pair(
-            table_ref, turned_ref, rank_ref, ordered_ref, permuted_ref, perms - rows_sent, i
-        ):
-            for c in range(block * columns // blocks, (block + 1) * columns // blocks):
-                total = square_ref[c * SUBLANES : (c + 1) * SUBLANES, :] + after
-                for r in range(0, LANES, 16):
-                    rows = pl.ds(pl.multiple_of((i * PAIR + u) * LANES + r, 16), 16)
-                    wide = genotypes_ref[rows, c * LANES : (c + 1) * LANES].astype(jnp.float32)
-                    wide = wide * wide
-                    total = total + (wide[:SUBLANES] + wide[SUBLANES:])
-                square_ref[c * SUBLANES : (c + 1) * SUBLANES, :] = total
-            after = value * 0.0
-        return carry
-
-    lax.fori_loop(0, chunks // PAIR, chunk_pair, 0)
+        for i in range(first, end):
+            for value in look_up_chunk(
+                table_ref, turned_ref, rank_ref, ordered_ref, permuted_ref, perms - rows_sent, i
+            ):
+                for item in work[done * len(work) // slots : (done + 1) * len(work) // slots]:
+                    add_squares(*item, after)
+                after = value * 0.0
+                done += 1
     square_row = (rows_sent + 1) * columns
     for c in range(columns):
         sent_ref[square_row + c : square_row + c + 1, :] = jnp.sum(
@@ -249,12 +259,9 @@
     chunks = permuted_ref.shape[1] // LANES
     fill_ranks(rank_ref)
 
-    def chunk_pair(i, carry):
-        for _ in look_up_pair(table_ref, turned_ref, rank_ref, ordered_ref, permuted_ref, first_row, i):
+    for i in range(chunks):
+        for _ in look_up_chunk(table_ref, turned_ref, rank_ref, ordered_ref, permuted_ref, first_row, i):
             pass
-        return carry
-
-    lax.fori_loop(0, chunks // PAIR, chunk_pair, 0)
     multiply(permuted_ref[...].astype(jnp.bfloat16), permuted_ref.shape[0], genotypes_ref, out_ref)
 
 

time: 29.8 us -> 28.7 us (0.963)
  Pallas kernels: 13.7 us -> 11.4 us
  waiting for transfers between devices: 5.89 us -> 7.16 us
    pallas_call x3, Pallas kernels: 7.83 us -> 5.76 us  [own_rows(): pl.pallas_call(functools.partial(rows_kernel, first_row), out_shape=jax.S...]
    ppermute x7, waiting for transfers between devices: 5.89 us -> 7.16 us  [on_device(): got.append(lax.ppermute(message, 'samp', pairs))]
  transfers between devices with their start and end apart: 8 -> 8, of which waited for: 4 -> 4; matrix products, arithmetic and copies ran while one was open for 0% -> 0% of each run, Pallas kernels for 26% -> 20%
where the time goes in v7:
time: 28.7 us; the launch traced here: 28.6 us
  Pallas kernels  11.4 us (40%)
  starting transfers between devices  9.18 us (32%)
  waiting for transfers between devices  7.16 us (25%)
  between operations  0.73 us (3%)
    ppermute x7, starting transfers between devices, on_device(): got.append(lax.ppermute(message, 'samp', pairs))  9.16 us
    ppermute x7, waiting for transfers between devices, on_device(): got.append(lax.ppermute(message, 'samp', pairs))  7.16 us
    pallas_call x3, Pallas kernels, own_rows(): pl.pallas_call(functools.partial(rows_kernel, first_row), out_shape=jax.S...  5.76 us
    pallas_call x1, Pallas kernels, on_device(): pl.pallas_call(functools.partial(head_kernel, devices, block_rows), out_s...  4.98 us
    pallas_call x1, Pallas kernels, on_device(): pl.pallas_call(functools.partial(final_kernel, samples), out_shape=(jax.S...  0.66 us
  transfers between devices with their start and end apart: 8, of which 4 were waited for; matrix products, arithmetic and copies ran while one was open for 0% of the time, Pallas kernels for 20%

profile of v7, /device:TPU:0, one launch (start us, length us, event | category | flops | bytes accessed | tf_op | source)
XLA Modules:
  0.0 28.6 jit_solution(554825324290976458)
XLA Ops:
  0.6 5.0 %shard_map.50 = (f32[416,128]{1,0:T(8,128)S(1)}, bf16[1024,2048]{1,0:T(8,128)(2,1)S(1)}, s32[64,1024]{1,0:T(8,128)S(1)}, s32[128,128]{1,0:T(8,128)S(1)}, bf16[12...) custom-call(f32[256,128]{1,0:T(8,128)} %bitcast.1, s32[64,1024]{1,0:T(8,128)} %index_hbm.1, bf16[1024,2048]{1,0:T(8,128)(2,1)} %genotypes_hbm.1), custom_call_target="tpu_custom_call" | custom-call | tf_op jit(solution)/shard_map/pallas_call | solution.py:303
  5.6 0.6 %collective-permute-start.1 = (f32[416,128]{1,0:T(8,128)S(1)}, f32[416,128]{1,0:T(8,128)S(1)}, u32[]{:S(2)}, u32[]{:S(2)}) collective-permute-start(f32[416,128]{1,0:T(8,128)S(1)} %get-tuple-element.13), channel_id=1, source_target_pairs={{0,1},{1,0},{2,3},{3,2},{4,5},{5,4},{6,7},{7,6},{8,9},{9,8},{10,11... | collective-permute-start | bytes 638984 | tf_op jit(solution)/shard_map/ppermute | solution.py:359
  6.2 3.0 %shard_map.53 = f32[384,128]{1,0:T(8,128)S(1)} custom-call(bf16[1024,2048]{1,0:T(8,128)(2,1)S(1)} %get-tuple-element.9.genotypes_ref, s32[64,1024]{1,0:T(8,128)S(1)} %get-tuple-element.10.ordered_ref, s32[128,128]{1,0:T(8,128)S(1)} %get-tuple-element.11.table_ref, bf16[128,256]{1,0:T(8,128)(2,1)S(1)} %get-tuple-element.12.turned_ref), custom_call_target="tpu_custom_call" | custom-call | flops 1711276032 | bytes 4194304 | tf_op jit(solution)/shard_map/pallas_call | solution.py:327
  9.2 0.0 collective-permute-done.1
  9.3 3.5 %collective-permute-start.4 = (f32[160,128]{1,0:T(8,128)S(1)}, f32[160,128]{1,0:T(8,128)S(1)}, u32[]{:S(2)}, u32[]{:S(2)}) collective-permute-start(f32[160,128]{1,0:T(8,128)S(1)} %get-tuple-element.26), channel_id=1, source_target_pairs={{0,6},{1,7},{2,4},{3,5},{4,2},{5,3},{6,0},{7,1},{8,14},{9,15},{10,... | collective-permute-start | bytes 245768 | tf_op jit(solution)/shard_map/ppermute | solution.py:359
  12.8 0.5 %collective-permute-start.3 = (f32[160,128]{1,0:T(8,128)S(1)}, f32[160,128]{1,0:T(8,128)S(1)}, u32[]{:S(2)}, u32[]{:S(2)}) collective-permute-start(f32[160,128]{1,0:T(8,128)S(1)} %get-tuple-element.25), channel_id=1, source_target_pairs={{0,2},{1,5},{2,0},{3,7},{4,6},{5,1},{6,4},{7,3},{8,10},{9,13},{10,... | collective-permute-start | bytes 245768 | tf_op jit(solution)/shard_map/ppermute | solution.py:359
  13.3 0.1 collective-permute-start.2
  13.4 1.4 %shard_map.52 = f32[128,128]{1,0:T(8,128)S(1)} custom-call(bf16[1024,2048]{1,0:T(8,128)(2,1)S(1)} %get-tuple-element.9.genotypes_ref, s32[64,1024]{1,0:T(8,128)S(1)} %get-tuple-element.10.ordered_ref, s32[128,128]{1,0:T(8,128)S(1)} %get-tuple-element.11.table_ref, bf16[128,256]{1,0:T(8,128)(2,1)S(1)} %get-tuple-element.12.turned_ref), custom_call_target="tpu_custom_call" | custom-call | flops 570425344 | bytes 4194304 | tf_op jit(solution)/shard_map/pallas_call | solution.py:327
  14.8 0.0 collective-permute-start
  14.8 1.4 %shard_map.51 = f32[128,128]{1,0:T(8,128)S(1)} custom-call(bf16[1024,2048]{1,0:T(8,128)(2,1)S(1)} %get-tuple-element.9.genotypes_ref, s32[64,1024]{1,0:T(8,128)S(1)} %get-tuple-element.10.ordered_ref, s32[128,128]{1,0:T(8,128)S(1)} %get-tuple-element.11.table_ref, bf16[128,256]{1,0:T(8,128)(2,1)S(1)} %get-tuple-element.12.turned_ref), custom_call_target="tpu_custom_call" | custom-call | flops 570425344 | bytes 4194304 | tf_op jit(solution)/shard_map/pallas_call | solution.py:327
  16.2 0.0 collective-permute-done
  16.2 0.0 collective-permute-done.4
  16.2 1.7 %collective-permute-done.3 = f32[160,128]{1,0:T(8,128)S(1)} collective-permute-done((f32[160,128]{1,0:T(8,128)S(1)}, f32[160,128]{1,0:T(8,128)S(1)}, u32[]{:S(2)}, u32[]{:S(2)}) %collective-permute-start.3) | collective-permute-done | bytes 81952 | tf_op jit(solution)/shard_map/ppermute | solution.py:359
  17.9 0.0 collective-permute-done.2
  18.0 2.7 %collective-permute-start.5 = (f32[64,128]{1,0:T(8,128)S(1)}, f32[64,128]{1,0:T(8,128)S(1)}, u32[]{:S(2)}, u32[]{:S(2)}) collective-permute-start(f32[64,128]{1,0:T(8,128)S(1)} %get-tuple-element.23), channel_id=1, source_target_pairs={{0,16},{1,17},{2,18},{3,19},{4,20},{5,21},{6,22},{7,23},{8,24},{9,... | collective-permute-start | bytes 98312 | tf_op jit(solution)/shard_map/ppermute | solution.py:359
  20.6 1.6 %collective-permute-start.6 = (f32[64,128]{1,0:T(8,128)S(1)}, f32[64,128]{1,0:T(8,128)S(1)}, u32[]{:S(2)}, u32[]{:S(2)}) collective-permute-start(f32[64,128]{1,0:T(8,128)S(1)} %get-tuple-element.22), channel_id=1, source_target_pairs={{0,8},{1,9},{2,10},{3,11},{4,12},{5,13},{6,14},{7,15},{8,0},{9,1},... | collective-permute-start | bytes 98312 | tf_op jit(solution)/shard_map/ppermute | solution.py:359
  22.2 0.2 collective-permute-start.7
  22.4 0.6 %collective-permute-done.5.refs_0_ = f32[64,128]{1,0:T(8,128)S(1)} collective-permute-done((f32[64,128]{1,0:T(8,128)S(1)}, f32[64,128]{1,0:T(8,128)S(1)}, u32[]{:S(2)}, u32[]{:S(2)}) %collective-permute-start.5) | collective-permute-done | bytes 32800 | tf_op jit(solution)/shard_map/ppermute | solution.py:359
  23.1 1.5 %collective-permute-done.6.refs_1_ = f32[64,128]{1,0:T(8,128)S(1)} collective-permute-done((f32[64,128]{1,0:T(8,128)S(1)}, f32[64,128]{1,0:T(8,128)S(1)}, u32[]{:S(2)}, u32[]{:S(2)}) %collective-permute-start.6) | collective-permute-done | bytes 32800 | tf_op jit(solution)/shard_map/ppermute | solution.py:359
  24.5 3.4 %collective-permute-done.7.refs_2_ = f32[64,128]{1,0:T(8,128)S(1)} collective-permute-done((f32[64,128]{1,0:T(8,128)S(1)}, f32[64,128]{1,0:T(8,128)S(1)}, u32[]{:S(2)}, u32[]{:S(2)}) %collective-permute-start.7) | collective-permute-done | bytes 32800 | tf_op jit(solution)/shard_map/ppermute | solution.py:359
  27.9 0.7 %shard_map.54 = (f32[2,2048]{1,0:T(2,128)}, f32[2]{0:T(128)}) custom-call(f32[8,128]{1,0:T(8,128)S(1)} %get-tuple-element.8.sigma2_ref, f32[32,128]{1,0:T(8,128)S(1)} %get-tuple-element.20.held_ref, f32[32,128]{1,0:T(8,128)S(1)} %slice_add_fusion.4.moments_ref, f32[64,128]{1,0:T(8,128)S(1)} %collective-permute-done.5.refs_0_, ...), custom_call_target="tpu_custom_call" | custom-call | tf_op jit(solution)/shard_map/pallas_call | solution.py:378
  (8 shorter events, 0.1 us)
Async XLA Ops:
  5.6 3.6 %collective-permute-start.1 = (f32[416,128]{1,0:T(8,128)S(1)}, f32[416,128]{1,0:T(8,128)S(1)}, u32[]{:S(2)}, u32[]{:S(2)}) collective-permute-start(f32[416,128]{1,0:T(8,128)S(1)} %get-tuple-element.13), channel_id=1, source_target_pairs={{0,1},{1,0},{2,3},{3,2},{4,5},{5,4},{6,7},{7,6},{8,9},{9,8},{10,11... | collective-permute-start | bytes 638984 | tf_op jit(solution)/shard_map/ppermute | solution.py:359
  9.3 7.0 %collective-permute-start.4 = (f32[160,128]{1,0:T(8,128)S(1)}, f32[160,128]{1,0:T(8,128)S(1)}, u32[]{:S(2)}, u32[]{:S(2)}) collective-permute-start(f32[160,128]{1,0:T(8,128)S(1)} %get-tuple-element.26), channel_id=1, source_target_pairs={{0,6},{1,7},{2,4},{3,5},{4,2},{5,3},{6,0},{7,1},{8,14},{9,15},{10,... | collective-permute-start | bytes 245768 | tf_op jit(solution)/shard_map/ppermute | solution.py:359
  12.8 5.1 %collective-permute-start.3 = (f32[160,128]{1,0:T(8,128)S(1)}, f32[160,128]{1,0:T(8,128)S(1)}, u32[]{:S(2)}, u32[]{:S(2)}) collective-permute-start(f32[160,128]{1,0:T(8,128)S(1)} %get-tuple-element.25), channel_id=1, source_target_pairs={{0,2},{1,5},{2,0},{3,7},{4,6},{5,1},{6,4},{7,3},{8,10},{9,13},{10,... | collective-permute-start | bytes 245768 | tf_op jit(solution)/shard_map/ppermute | solution.py:359
  13.3 4.6 %collective-permute-start.2 = (f32[160,128]{1,0:T(8,128)S(1)}, f32[160,128]{1,0:T(8,128)S(1)}, u32[]{:S(2)}, u32[]{:S(2)}) collective-permute-start(f32[160,128]{1,0:T(8,128)S(1)} %get-tuple-element.24), channel_id=1, source_target_pairs={{0,4},{1,3},{2,6},{3,1},{4,0},{5,7},{6,2},{7,5},{8,12},{9,11},{10,... | collective-permute-start | bytes 245768 | tf_op jit(solution)/shard_map/ppermute | solution.py:359
  14.8 1.4 %collective-permute-start = (f32[128,128]{1,0:T(8,128)S(1)}, f32[128,128]{1,0:T(8,128)S(1)}, u32[]{:S(2)}, u32[]{:S(2)}) collective-permute-start(f32[128,128]{1,0:T(8,128)S(1)} %shard_map.52), channel_id=1, source_target_pairs={{0,1},{1,0},{2,3},{3,2},{4,5},{5,4},{6,7},{7,6},{8,9},{9,8},{10,11... | collective-permute-start | bytes 196616 | tf_op jit(solution)/shard_map/ppermute | solution.py:367
  18.0 5.1 %collective-permute-start.5 = (f32[64,128]{1,0:T(8,128)S(1)}, f32[64,128]{1,0:T(8,128)S(1)}, u32[]{:S(2)}, u32[]{:S(2)}) collective-permute-start(f32[64,128]{1,0:T(8,128)S(1)} %get-tuple-element.23), channel_id=1, source_target_pairs={{0,16},{1,17},{2,18},{3,19},{4,20},{5,21},{6,22},{7,23},{8,24},{9,... | collective-permute-start | bytes 98312 | tf_op jit(solution)/shard_map/ppermute | solution.py:359
  20.6 3.9 %collective-permute-start.6 = (f32[64,128]{1,0:T(8,128)S(1)}, f32[64,128]{1,0:T(8,128)S(1)}, u32[]{:S(2)}, u32[]{:S(2)}) collective-permute-start(f32[64,128]{1,0:T(8,128)S(1)} %get-tuple-element.22), channel_id=1, source_target_pairs={{0,8},{1,9},{2,10},{3,11},{4,12},{5,13},{6,14},{7,15},{8,0},{9,1},... | collective-permute-start | bytes 98312 | tf_op jit(solution)/shard_map/ppermute | solution.py:359
  22.2 5.7 %collective-permute-start.7 = (f32[64,128]{1,0:T(8,128)S(1)}, f32[64,128]{1,0:T(8,128)S(1)}, u32[]{:S(2)}, u32[]{:S(2)}) collective-permute-start(f32[64,128]{1,0:T(8,128)S(1)} %get-tuple-element.21), channel_id=1, source_target_pairs={{0,24},{1,25},{2,26},{3,27},{4,28},{5,29},{6,30},{7,31},{8,16},{9,... | collective-permute-start | bytes 98312 | tf_op jit(solution)/shard_map/ppermute | solution.py:359
